TPU v7x, 768 devices: a whole 4x8x12 slice. The times are simulated.
768 devices in a mesh: batch: 8 (over y), dir: 96 (over z, x, core).
Axes of the slice: x: 4, y: 8, z: 12, core: 2. Of those that a mesh axis runs over, the one named last changes fastest.
Arguments:
- embeddings: bfloat16 [3072, 2048], P(('batch', 'dir')), may hold values from -13 to 13
- directions: bfloat16 [2048, 24576], P(None, 'dir'), may hold values from -0.125 to 0.125
Outputs:
- grad_embed: float32 [3072, 2048], P(('batch', 'dir'))
All inputs are finite; a program needn't handle non-finite values.
Results may differ from a plain program's by a relative error of at most 0.0016.
Values may be sent and summed in bfloat16 or wider, within the bound.
No kernel may reach another device: no remote copies, remote signals or barrier semaphores. Data moves between devices by JAX's collectives and lax.ppermute only.
A program may use at most 32 MiB of HBM per device.

v0:
```python
import jax
import jax.numpy as jnp
from jax import lax
from jax.sharding import PartitionSpec as P

KNOTS = 17


def knot_table():
    index = jnp.arange(KNOTS, dtype=jnp.float32)
    spacing = 3.0 / (KNOTS - 1)
    knot_pos = index * spacing
    target = jnp.exp(-0.5 * knot_pos * knot_pos)
    ends = jnp.where((index == 0) | (index == KNOTS - 1), 0.5, 1.0)
    weights = ends * spacing * target
    return (knot_pos, weights, target)


def local(embeddings, directions):
    dir_float = directions.astype(jnp.float32)
    unit = (
        dir_float / jnp.sqrt(jnp.sum(dir_float * dir_float, axis=0, keepdims=True) + 1e-06)
    ).astype(jnp.bfloat16)
    projected = jnp.dot(
        lax.all_gather(embeddings, "dir", axis=0, tiled=True),
        unit,
        preferred_element_type=jnp.float32,
    )
    total_rows = embeddings.shape[0] * lax.axis_size("dir") * lax.axis_size("batch")
    knot_pos, weights, target = knot_table()
    angles = knot_pos[:, None, None] * projected[None]
    cosine_vals = jnp.cos(angles)
    sine_vals = jnp.sin(angles)
    cos_part = jnp.sum(cosine_vals, axis=1)
    sin_part = jnp.sum(sine_vals, axis=1)
    cos_total, sin_total = lax.psum((cos_part, sin_part), "batch")
    cos_mean = cos_total / total_rows
    sin_mean = sin_total / total_rows
    cos_coef = 2.0 * weights[:, None] * (cos_mean - target[:, None])
    sin_coef = 2.0 * weights[:, None] * sin_mean
    grad_proj = jnp.sum(
        knot_pos[:, None, None]
        * (cosine_vals * sin_coef[:, None, :] - sine_vals * cos_coef[:, None, :]),
        axis=0,
    ).astype(jnp.bfloat16)
    return lax.psum_scatter(
        lax.dot_general(
            grad_proj, unit, (((1,), (1,)), ((), ())), preferred_element_type=jnp.float32
        ),
        "dir",
        scatter_dimension=0,
        tiled=True,
    )


def solution(mesh):
    placed = (P(("batch", "dir"), None), P(None, "dir"))
    return jax.shard_map(
        local, mesh=mesh, in_specs=placed, out_specs=P(("batch", "dir"), None), check_vma=False
    )
```

profile of v0, /device:TPU:6, one launch (start us, length us, event | category | flops | bytes accessed | tf_op | source)
XLA Modules:
  0.0 511.3 jit_solution(12865339291521535483)
XLA Ops:
  6.5 0.0 copy-start
  6.5 0.0 all-gather.3.cloned.1.call-start
  6.5 0.7 all-gather.3.cloned.1.call-update
  7.3 0.0 all-reduce.4.cloned.1.call-start
  7.4 1.5 fusion.7
  8.9 124.4 %all-gather.3.cloned.1.call-done = bf16[96,4,2048]{2,1,0:T(4,128)(2,1)} async-done(((bf16[1,4,2048]{2,1,0:T(4,128)(2,1)}), bf16[96,4,2048]{2,1,0:T(4,128)(2,1)}) %all-gather.3.cloned.1.call-update) | async-done | bytes 1572880 | tf_op jit(solution)/shard_map/all_gather | solution.py:25
  133.3 2.3 reshape.34
  135.7 0.0 copy-done
  135.7 0.7 convolution_bitcast_fusion
  136.5 0.2 copy.5
  136.6 24.3 %fusion.3 = (f32[17,256]{1,0:T(8,128)S(1)}, f32[17,256]{1,0:T(8,128)S(1)}) fusion(f32[384,256]{1,0:T(8,128)S(1)} %copy.5, f32[17]{0:T(128)S(1)} %iota_multiply_fusion.1), kind=kLoop, calls=%fused_computation.5 | loop fusion | flops 5004800 | bytes 428100 | tf_op jit(solution)/shard_map/reduce_sum | solution.py:35
  161.0 30.2 %all-reduce.1 = (f32[17,256]{1,0:T(8,128)S(1)}, f32[17,256]{1,0:T(8,128)S(1)}) all-reduce(f32[17,256]{1,0:T(8,128)S(1)} %get-tuple-element.6, f32[17,256]{1,0:T(8,128)S(1)} %get-tuple-element.5), channel_id=1, replica_groups=mesh['batch'=8,'dir'=96] {'batch'}, use_global_device_ids=true, to_apply=%region_4.5 | all-reduce | flops 8704 | bytes 69632 | tf_op jit(solution)/shard_map/psum | solution.py:36
  191.2 0.1 subtract_multiply_fusion
  191.2 24.5 %fusion.6 = bf16[384,256]{1,0:T(8,128)(2,1)S(1)} fusion(f32[17,256]{1,0:T(8,128)S(1)} %get-tuple-element.9, f32[17,256]{1,0:T(8,128)S(1)} %get-tuple-element.10, f32[384,256]{1,0:T(8,128)S(1)} %copy.5, f32[17]{0:T(128)S(1)} %iota_multiply_fusion.1), kind=kLoop, calls=%fused_computation.8 | loop fusion | flops 9928704 | bytes 624708 | tf_op jit(solution)/shard_map/reduce_sum | solution.py:41
  215.8 2.3 fusion.9
  218.1 0.0 all-reduce.4.cloned.1.call-update
  218.1 1.3 dynamic-slice
  220.1 283.0 %all-reduce.4.cloned.1.call-done = f32[384,2048]{1,0:T(8,128)} async-done(((f32[384,2048]{1,0:T(8,128)}), f32[384,2048]{1,0:T(8,128)}) %all-reduce.4.cloned.1.call-update) | async-done | bytes 3145744
  503.0 1.5 constant_dynamic-slice_fusion
  (5 shorter events, 0.1 us)
Async XLA Ops:
  6.5 129.2 %copy-start = (bf16[2048,256]{1,0:T(8,128)(2,1)S(1)}, bf16[2048,256]{1,0:T(8,128)(2,1)}, u32[]{:S(2)}) copy-start(bf16[2048,256]{1,0:T(8,128)(2,1)} %param.3) | copy-start | bytes 3145732
  6.5 126.8 %all-gather.3.cloned.1.call-start = ((), (), s32[]{:S(2)}) async-start(), calls=%async_computation | async-start | bytes 1589248 | tf_op jit(solution)/shard_map/all_gather | solution.py:25
  7.3 495.8 %all-reduce.4.cloned.1.call-start = ((), (), s32[]{:S(2)}) async-start(), calls=%async_computation.1 | async-start | bytes 6291456
Sparse Core Ops, SparseCore 0:
  11.0 122.2 all-gather.2
  218.2 284.7 all-reduce.3
where the time goes:
time: 512 us; the launch traced here: 511 us
  waiting for transfers between devices  408 us (80%)
  other arithmetic  50.5 us (10%)
  blocking collectives  30.2 us (6%)
  between operations  14.1 us (3%)
  local copies, waits for them, and re-layouts  5.25 us (1%)
    unnamed x3, waiting for transfers between devices  284 us
    all_gather x1, waiting for transfers between devices, local(): lax.all_gather(embeddings, 'dir', axis=0, tiled=True)  124 us
    psum x1, blocking collectives, local(): cos_total, sin_total = lax.psum((cos_part, sin_part), 'batch')  30.2 us
    reduce_sum x1, other arithmetic, local(): jnp.sum(knot_pos[:, None, None] * (cosine_vals * sin_coef[:, None, :] - s...  24.5 us
    reduce_sum x1, other arithmetic, local(): sin_part = jnp.sum(sine_vals, axis=1)  24.3 us
  transfers between devices with their start and end apart: 2, of which 2 were waited for; matrix products, arithmetic and copies ran while one was open for 1% of the time, Pallas kernels for 0%

commit v1 on v0

v1 whole, which is shorter than its diff:
```python
import math

import jax
import jax.numpy as jnp
from jax import lax
from jax.experimental import pallas as pl
from jax.experimental.pallas import tpu as pltpu
from jax.sharding import Mesh, PartitionSpec as P

KNOTS = 17
STEP = 3.0 / (KNOTS - 1)
KNOT = [k * STEP for k in range(KNOTS)]
TARGET = [math.exp(-0.5 * t * t) for t in KNOT]
WEIGHT = [(0.5 if k in (0, KNOTS - 1) else 1.0) * STEP * TARGET[k] for k in range(KNOTS)]
TURN = (6.28125, 0.0019340515136719, 1.2556659146e-06)
TILE = 32
F32 = jnp.float32
BF16 = jnp.bfloat16


def base_angle(proj):
    theta = proj * STEP
    turns = jnp.round(theta * (0.5 / math.pi))
    q = 0.25 * (((theta - turns * TURN[0]) - turns * TURN[1]) - turns * TURN[2])
    z = q * q
    s = q * (1.0 + z * (-1.0 / 6 + z * (1.0 / 120 + z * (-1.0 / 5040 + z * (1.0 / 362880)))))
    c = 1.0 - z * (0.5 + z * (-1.0 / 24 + z * (1.0 / 720 + z * (-1.0 / 40320))))
    s2 = 2.0 * s * c
    c2 = 1.0 - 2.0 * s * s
    return 1.0 - 2.0 * s2 * s2, 2.0 * s2 * c2


def unit_kernel(dir_ref, unit_ref):
    width = dir_ref.shape[1]
    rows = 256
    total = jnp.zeros((8, width), F32)
    for i in range(dir_ref.shape[0] // rows):
        w = dir_ref[pl.ds(i * rows, rows), :].astype(F32)
        total = total + jnp.sum((w * w).reshape(rows // 8, 8, width), axis=0)
    inv = 1.0 / jnp.sqrt(jnp.sum(total, axis=0, keepdims=True) + 1e-06)
    for i in range(dir_ref.shape[0] // rows):
        w = dir_ref[pl.ds(i * rows, rows), :].astype(F32)
        unit_ref[pl.ds(i * rows, rows), :] = (w * inv).astype(BF16)


def sums_kernel(mine_ref, other_ref, unit_ref, c_ref, s_ref, out_ref, proj_ref, acc_ref):
    half = mine_ref.shape[0]
    rows, width = proj_ref.shape
    proj_ref[pl.ds(0, half), :] = jnp.dot(mine_ref[...], unit_ref[...], preferred_element_type=F32)
    proj_ref[pl.ds(half, half), :] = jnp.dot(other_ref[...], unit_ref[...], preferred_element_type=F32)
    acc_ref[...] = jnp.zeros_like(acc_ref)

    def fold(v):
        return jnp.sum(v.reshape(TILE // 8, 8, width), axis=0)

    @pl.loop(0, rows // TILE)
    def _(i):
        at = pl.ds(pl.multiple_of(i * TILE, TILE), TILE)
        c1, s1 = base_angle(proj_ref[at, :])
        c_ref[at, :] = c1
        s_ref[at, :] = s1
        two = c1 + c1
        acc_ref[0] += fold(c1)
        acc_ref[KNOTS - 1] += fold(s1)
        cp, sp, cc, sc = jnp.ones_like(c1), jnp.zeros_like(c1), c1, s1
        for k in range(1, KNOTS - 1):
            cp, cc = cc, two * cc - cp
            sp, sc = sc, two * sc - sp
            acc_ref[k] += fold(cc)
            acc_ref[KNOTS - 1 + k] += fold(sc)

    sums = jnp.sum(acc_ref[...], axis=1)
    for i in range(out_ref.shape[0]):
        out_ref[i] = sums


def grad_kernel(total_rows, c_ref, s_ref, sums_ref, unit_ref, mine_ref, out_ref, g_ref, rep_ref):
    rows, width = c_ref.shape
    half = rows // 2
    sums = jnp.sum(sums_ref[...], axis=0)
    for k in range(KNOTS):
        if k == 0:
            cos_total = jnp.full((1, width), total_rows, F32)
            sin_total = jnp.zeros((1, width), F32)
        else:
            cos_total = sums[k - 1 : k]
            sin_total = sums[KNOTS + k - 2 : KNOTS + k - 1]
        cos_coef = 2.0 * WEIGHT[k] * (cos_total / total_rows - TARGET[k])
        sin_coef = 2.0 * WEIGHT[k] * (sin_total / total_rows)
        rep_ref[k] = jnp.broadcast_to(KNOT[k] * sin_coef, (8, width))
        rep_ref[KNOTS + k] = jnp.broadcast_to(-KNOT[k] * cos_coef, (8, width))

    @pl.loop(0, rows // TILE)
    def _(i):
        at = pl.ds(pl.multiple_of(i * TILE, TILE), TILE)
        c1 = c_ref[at, :].reshape(TILE // 8, 8, width)
        s1 = s_ref[at, :].reshape(TILE // 8, 8, width)
        two = c1 + c1
        a2 = jnp.zeros_like(c1)
        b2 = a2
        a1 = rep_ref[KNOTS - 1] + a2
        b1 = rep_ref[2 * KNOTS - 1] + a2
        for k in range(KNOTS - 2, 0, -1):
            a1, a2 = rep_ref[k] + (two * a1 - a2), a1
            b1, b2 = rep_ref[KNOTS + k] + (two * b1 - b2), b1
        g = rep_ref[0] + (c1 * a1 - a2) + s1 * b1
        g_ref[at, :] = g.reshape(TILE, width).astype(BF16)

    mine_ref[...] = g_ref[pl.ds(0, half), :]
    times_unit(g_ref.at[pl.ds(half, half), :], unit_ref, out_ref)


def times_unit(g_ref, unit_ref, out_ref):
    step = 512
    for j in range(unit_ref.shape[0] // step):
        at = pl.ds(j * step, step)
        out_ref[:, at] = lax.dot_general(
            g_ref[...], unit_ref[at, :], (((1,), (1,)), ((), ())), preferred_element_type=F32
        )


def call(kernel, outs, scratch, flops, moved, operands):
    whole = pl.BlockSpec(memory_space=pltpu.VMEM)
    return pl.pallas_call(
        kernel,
        out_shape=outs,
        in_specs=[whole] * operands,
        out_specs=jax.tree.map(lambda _: whole, outs),
        scratch_shapes=scratch,
        compiler_params=pltpu.CompilerParams(vmem_limit_bytes=16 << 20),
        cost_estimate=pl.CostEstimate(flops=flops, bytes_accessed=moved, transcendentals=0),
    )


def to_all(x, axes, peers):
    return lax.all_to_all(jnp.broadcast_to(x[None], (peers,) + x.shape), axes, 0, 0, tiled=True)


def local(embeddings, directions):
    near, far, batch = lax.axis_size(("zl", "x")), lax.axis_size("zh"), lax.axis_size("y")
    swap = [(0, 1), (1, 0)]
    depth, width = directions.shape
    rows = embeddings.shape[0] * near * far
    total_rows = float(2 * rows * batch)
    sds = jax.ShapeDtypeStruct

    gathered = to_all(embeddings, "zh", far).reshape(-1, depth)
    mine = to_all(gathered, ("zl", "x"), near).reshape(rows, depth)
    other = lax.ppermute(mine, "c", swap)
    unit = call(unit_kernel, sds((depth, width), BF16), (), 4 * depth * width, 4 * depth * width, 1)(directions)

    c1, s1, sums = call(
        sums_kernel,
        (sds((2 * rows, width), F32), sds((2 * rows, width), F32), sds((batch, 2 * KNOTS - 2, width), F32)),
        (pltpu.VMEM((2 * rows, width), F32), pltpu.VMEM((2 * KNOTS - 2, 8, width), F32)),
        4 * rows * depth * width,
        8 * rows * depth,
        3,
    )(mine, other, unit)
    sums = lax.all_to_all(sums, "y", 0, 0, tiled=True)

    def grad(*refs):
        grad_kernel(total_rows, *refs)

    kept, theirs = call(
        grad,
        (sds((rows, width), BF16), sds((rows, depth), F32)),
        (pltpu.VMEM((2 * rows, width), BF16), pltpu.VMEM((2 * KNOTS, 8, width), F32)),
        2 * rows * depth * width,
        4 * rows * depth,
        4,
    )(c1, s1, sums, unit)
    arrived = lax.ppermute(theirs, "c", swap)
    ours = call(times_unit, sds((rows, depth), F32), (), 2 * rows * depth * width, 4 * rows * depth, 2)(kept, unit)
    part = (ours + arrived).astype(BF16).reshape(near, rows // near, depth)
    part = lax.all_to_all(part, ("zl", "x"), 0, 0, tiled=True)
    part = jnp.sum(part.astype(F32), axis=0).reshape(far, -1, depth)
    part = lax.all_to_all(part, "zh", 0, 0, tiled=True)
    return jnp.sum(part, axis=0)


def solution(mesh):
    fine = Mesh(mesh.devices.reshape(8, 4, 3, 4, 2), ("y", "zh", "zl", "x", "c"))
    along = ("zh", "zl", "x", "c")
    rows = P(("y",) + along, None)
    return jax.shard_map(local, mesh=fine, in_specs=(rows, P(None, along)), out_specs=rows, check_vma=False)
```

time: 512 us -> 115 us (0.22)
  waiting for transfers between devices: 408 us -> 4.85 us
  blocking collectives: 30.2 us -> 98.7 us
  other arithmetic: 50.5 us -> 0.93 us
  between operations: 14.1 us -> 0.07 us
    unnamed x3 -> x0, waiting for transfers between devices: 284 us -> none
    all_gather x1 -> x0, waiting for transfers between devices: 124 us -> none  [local(): lax.all_gather(embeddings, 'dir', axis=0, tiled=True)]
    all_to_all x0 -> x5, blocking collectives: none -> 98.7 us  [the longest x2 44 us: to_all(): lax.all_to_all(jnp.broadcast_to(x[None], (peers,) + x.shape), axes, 0, 0,...]
    reduce_sum x3 -> x2, other arithmetic: 50.4 us -> 0.76 us  [the longest x1 0.64 us: local(): return jnp.sum(part, axis=0)]
    psum x1 -> x0, blocking collectives: 30.2 us -> none  [local(): cos_total, sin_total = lax.psum((cos_part, sin_part), 'batch')]
  transfers between devices with their start and end apart: 2 -> 2, of which waited for: 2 -> 2; matrix products, arithmetic and copies ran while one was open for 1% -> 0% of each run, Pallas kernels for 0% -> 1%
where the time goes in v1:
time: 115 us; the launch traced here: 114 us
  blocking collectives  98.7 us (86%)
  Pallas kernels  5.02 us (4%)
  waiting for transfers between devices  4.85 us (4%)
  starting transfers between devices  3.83 us (3%)
    all_to_all x2, blocking collectives, to_all(): lax.all_to_all(jnp.broadcast_to(x[None], (peers,) + x.shape), axes, 0, 0,...  44 us
    all_to_all x1, blocking collectives, local(): part = lax.all_to_all(part, ('zl', 'x'), 0, 0, tiled=True)  19.4 us
    all_to_all x1, blocking collectives, local(): sums = lax.all_to_all(sums, 'y', 0, 0, tiled=True)  19.1 us
    all_to_all x1, blocking collectives, local(): part = lax.all_to_all(part, 'zh', 0, 0, tiled=True)  16.1 us
    ppermute x1, waiting for transfers between devices, local(): arrived = lax.ppermute(theirs, 'c', swap)  2.88 us
    pallas_call x1, Pallas kernels, local(): call(sums_kernel, (sds((2 * rows, width), F32), sds((2 * rows, width), F3...  2.36 us
  transfers between devices with their start and end apart: 2, of which 2 were waited for; matrix products, arithmetic and copies ran while one was open for 0% of the time, Pallas kernels for 1%

profile of v1, /device:TPU:6, one launch (start us, length us, event | category | flops | bytes accessed | tf_op | source)
XLA Modules:
  0.0 114.4 jit_solution(10223656230368468508)
XLA Ops:
  0.0 0.0 copy-start
  0.0 0.8 broadcast_in_dim.6
  0.8 25.1 %all_to_all.25 = bf16[4,4,2048]{2,1,0:T(4,128)(2,1)S(1)} all-to-all(bf16[4,4,2048]{2,1,0:T(4,128)(2,1)S(1)} %broadcast_in_dim.6), channel_id=1, replica_groups=mesh['y'=8,'zh'=4,'zl'=3,'x'=4,'c'=2] {'zh'}, dimensions={0} | all-to-all | bytes 131072 | tf_op jit(solution)/shard_map/all_to_all | solution.py:136
  25.9 0.1 broadcast_in_dim.15
  26.0 19.0 %all_to_all.26 = bf16[12,16,2048]{2,1,0:T(8,128)(2,1)S(1)} all-to-all(bf16[12,16,2048]{2,1,0:T(8,128)(2,1)S(1)} %broadcast_in_dim.15), channel_id=1, replica_groups=mesh['y'=8,'zh'=4,'zl'=3,'x'=4,'c'=2] {'zl','x'}, dimensions={0} | all-to-all | bytes 1572864 | tf_op jit(solution)/shard_map/all_to_all | solution.py:136
  45.0 1.9 %collective-permute-start = (bf16[192,2048]{1,0:T(8,128)(2,1)S(1)}, bf16[192,2048]{1,0:T(8,128)(2,1)S(1)}, u32[]{:S(2)}, u32[]{:S(2)}) collective-permute-start(bf16[192,2048]{1,0:T(8,128)(2,1)S(1)} %bitcast.2), channel_id=1, source_target_pairs={{0,1},{1,0},{2,3},{3,2},{4,5},{5,4},{6,7},{7,6},{8,9},{9,8},{10,11... | collective-permute-start | bytes 2359304 | tf_op jit(solution)/shard_map/ppermute | solution.py:149
  46.9 0.0 copy-done
  46.9 0.3 shard_map.28.unit_ref.refs_3_
  47.2 2.0 %collective-permute-done.other_ref = bf16[192,2048]{1,0:T(8,128)(2,1)S(1)} collective-permute-done((bf16[192,2048]{1,0:T(8,128)(2,1)S(1)}, bf16[192,2048]{1,0:T(8,128)(2,1)S(1)}, u32[]{:S(2)}, u32[]{:S(2)}) %collective-permute-start) | collective-permute-done | bytes 786464 | tf_op jit(solution)/shard_map/ppermute | solution.py:149
  49.1 2.4 %shard_map.29 = (f32[384,256]{1,0:T(8,128)S(1)}, f32[384,256]{1,0:T(8,128)S(1)}, f32[8,32,256]{2,1,0:T(8,128)S(1)}) custom-call(bf16[192,2048]{1,0:T(8,128)(2,1)S(1)} %bitcast.3, bf16[192,2048]{1,0:T(8,128)(2,1)S(1)} %collective-permute-done.other_ref, bf16[2048,256]{1,0:T(8,128)(2,1)S(1)} %shard_map.28.unit_ref.refs_3_), custom_call_target="tpu_custom_call" | custom-call | flops 402653184 | bytes 3145728 | tf_op jit(solution)/shard_map/pallas_call | solution.py:152
  51.5 19.1 %all_to_all.27.refs_2_ = f32[8,32,256]{2,1,0:T(8,128)S(1)} all-to-all(f32[8,32,256]{2,1,0:T(8,128)S(1)} %get-tuple-element.12), channel_id=1, replica_groups=mesh['y'=8,'zh'=4,'zl'=3,'x'=4,'c'=2] {'y'}, dimensions={0} | all-to-all | bytes 524288 | tf_op jit(solution)/shard_map/all_to_all | solution.py:160
  70.6 1.9 %shard_map.30 = (bf16[192,256]{1,0:T(8,128)(2,1)S(1)}, f32[192,2048]{1,0:T(8,128)S(1)}) custom-call(f32[384,256]{1,0:T(8,128)S(1)} %get-tuple-element.10.refs_0_, f32[384,256]{1,0:T(8,128)S(1)} %get-tuple-element.11.refs_1_, f32[8,32,256]{2,1,0:T(8,128)S(1)} %all_to_all.27.refs_2_, bf16[2048,256]{1,0:T(8,128)(2,1)S(1)} %shard_map.28.unit_ref.refs_3_), custom_call_target="tpu_custom_call" | custom-call | flops 201326592 | bytes 1572864 | tf_op jit(solution)/shard_map/pallas_call | solution.py:165
  72.5 1.9 %collective-permute-start.1 = (f32[192,2048]{1,0:T(8,128)S(1)}, f32[192,2048]{1,0:T(8,128)S(1)}, u32[]{:S(2)}, u32[]{:S(2)}) collective-permute-start(f32[192,2048]{1,0:T(8,128)S(1)} %get-tuple-element.14), channel_id=1, source_target_pairs={{0,1},{1,0},{2,3},{3,2},{4,5},{5,4},{6,7},{7,6},{8,9},{9,8},{10,11... | collective-permute-start | bytes 4718600 | tf_op jit(solution)/shard_map/ppermute | solution.py:173
  74.4 0.5 shard_map.31
  74.9 2.9 %collective-permute-done.1 = f32[192,2048]{1,0:T(8,128)S(1)} collective-permute-done((f32[192,2048]{1,0:T(8,128)S(1)}, f32[192,2048]{1,0:T(8,128)S(1)}, u32[]{:S(2)}, u32[]{:S(2)}) %collective-permute-start.1) | collective-permute-done | bytes 1572896 | tf_op jit(solution)/shard_map/ppermute | solution.py:173
  77.8 0.2 add_convert_fusion
  78.0 19.4 %all_to_all.28 = bf16[12,16,2048]{2,1,0:T(8,128)(2,1)S(1)} all-to-all(bf16[12,16,2048]{2,1,0:T(8,128)(2,1)S(1)} %bitcast.4), channel_id=1, replica_groups=mesh['y'=8,'zh'=4,'zl'=3,'x'=4,'c'=2] {'zl','x'}, dimensions={0} | all-to-all | bytes 1572864 | tf_op jit(solution)/shard_map/all_to_all | solution.py:176
  97.4 0.1 convert_reduce_fusion
  97.6 16.1 %all_to_all.29 = f32[4,4,2048]{2,1,0:T(4,128)S(1)} all-to-all(f32[4,4,2048]{2,1,0:T(4,128)S(1)} %reshape.13), channel_id=1, replica_groups=mesh['y'=8,'zh'=4,'zl'=3,'x'=4,'c'=2] {'zh'}, dimensions={0} | all-to-all | bytes 262144 | tf_op jit(solution)/shard_map/all_to_all | solution.py:178
  113.7 0.6 reduce_sum.19
  (2 shorter events, 0.1 us)
Async XLA Ops:
  0.0 46.9 %copy-start = (bf16[2048,256]{1,0:T(8,128)(2,1)S(1)}, bf16[2048,256]{1,0:T(8,128)(2,1)}, u32[]{:S(2)}) copy-start(bf16[2048,256]{1,0:T(8,128)(2,1)} %dir_ref.1) | copy-start | bytes 3145732
  45.0 4.2 %collective-permute-start = (bf16[192,2048]{1,0:T(8,128)(2,1)S(1)}, bf16[192,2048]{1,0:T(8,128)(2,1)S(1)}, u32[]{:S(2)}, u32[]{:S(2)}) collective-permute-start(bf16[192,2048]{1,0:T(8,128)(2,1)S(1)} %bitcast.2), channel_id=1, source_target_pairs={{0,1},{1,0},{2,3},{3,2},{4,5},{5,4},{6,7},{7,6},{8,9},{9,8},{10,11... | collective-permute-start | bytes 2359304 | tf_op jit(solution)/shard_map/ppermute | solution.py:149
  72.5 5.3 %collective-permute-start.1 = (f32[192,2048]{1,0:T(8,128)S(1)}, f32[192,2048]{1,0:T(8,128)S(1)}, u32[]{:S(2)}, u32[]{:S(2)}) collective-permute-start(f32[192,2048]{1,0:T(8,128)S(1)} %get-tuple-element.14), channel_id=1, source_target_pairs={{0,1},{1,0},{2,3},{3,2},{4,5},{5,4},{6,7},{7,6},{8,9},{9,8},{10,11... | collective-permute-start | bytes 4718600 | tf_op jit(solution)/shard_map/ppermute | solution.py:173

commit v2 on v1

--- a/solution.py
+++ b/solution.py
@@ -1,3 +1,4 @@
+import functools
 import math
 
 import jax
@@ -16,6 +17,7 @@
 TILE = 32
 F32 = jnp.float32
 BF16 = jnp.bfloat16
+LINK = jnp.float16
 
 
 def base_angle(proj):
@@ -43,7 +45,7 @@
         unit_ref[pl.ds(i * rows, rows), :] = (w * inv).astype(BF16)
 
 
-def sums_kernel(mine_ref, other_ref, unit_ref, c_ref, s_ref, out_ref, proj_ref, acc_ref):
+def sums_kernel(local_rows, mine_ref, other_ref, unit_ref, c_ref, s_ref, out_ref, proj_ref, acc_ref):
     half = mine_ref.shape[0]
     rows, width = proj_ref.shape
     proj_ref[pl.ds(0, half), :] = jnp.dot(mine_ref[...], unit_ref[...], preferred_element_type=F32)
@@ -69,9 +71,9 @@
             acc_ref[k] += fold(cc)
             acc_ref[KNOTS - 1 + k] += fold(sc)
 
-    sums = jnp.sum(acc_ref[...], axis=1)
-    for i in range(out_ref.shape[0]):
-        out_ref[i] = sums
+    out_ref[...] = jnp.sum(acc_ref[...], axis=1)
+    for k in range(1, KNOTS):
+        out_ref[pl.ds(k - 1, 1), :] -= local_rows * TARGET[k]
 
 
 def grad_kernel(total_rows, c_ref, s_ref, sums_ref, unit_ref, mine_ref, out_ref, g_ref, rep_ref):
@@ -80,12 +82,12 @@
     sums = jnp.sum(sums_ref[...], axis=0)
     for k in range(KNOTS):
         if k == 0:
-            cos_total = jnp.full((1, width), total_rows, F32)
+            cos_off = jnp.full((1, width), total_rows * (1.0 - TARGET[0]), F32)
             sin_total = jnp.zeros((1, width), F32)
         else:
-            cos_total = sums[k - 1 : k]
+            cos_off = sums[k - 1 : k]
             sin_total = sums[KNOTS + k - 2 : KNOTS + k - 1]
-        cos_coef = 2.0 * WEIGHT[k] * (cos_total / total_rows - TARGET[k])
+        cos_coef = 2.0 * WEIGHT[k] * (cos_off / total_rows)
         sin_coef = 2.0 * WEIGHT[k] * (sin_total / total_rows)
         rep_ref[k] = jnp.broadcast_to(KNOT[k] * sin_coef, (8, width))
         rep_ref[KNOTS + k] = jnp.broadcast_to(-KNOT[k] * cos_coef, (8, width))
@@ -136,51 +138,55 @@
     return lax.all_to_all(jnp.broadcast_to(x[None], (peers,) + x.shape), axes, 0, 0, tiled=True)
 
 
+def turn(x, axis, by):
+    n = lax.axis_size(axis)
+    return lax.ppermute(x, axis, [(i, (i + by) % n) for i in range(n)])
+
+
 def local(embeddings, directions):
-    near, far, batch = lax.axis_size(("zl", "x")), lax.axis_size("zh"), lax.axis_size("y")
-    swap = [(0, 1), (1, 0)]
+    ring, along_x, batch = lax.axis_size("z"), lax.axis_size("x"), lax.axis_size("y")
     depth, width = directions.shape
-    rows = embeddings.shape[0] * near * far
+    block = embeddings.shape[0] * ring
+    rows = block * along_x
     total_rows = float(2 * rows * batch)
     sds = jax.ShapeDtypeStruct
 
-    gathered = to_all(embeddings, "zh", far).reshape(-1, depth)
-    mine = to_all(gathered, ("zl", "x"), near).reshape(rows, depth)
-    other = lax.ppermute(mine, "c", swap)
+    held = to_all(embeddings, "z", ring).reshape(block, depth)
+    far = [turn(held, "x", by) for by in (2, 1, along_x - 1)]
+    mine = jnp.concatenate([held] + far, axis=0)
+    other = turn(mine, "c", 1)
     unit = call(unit_kernel, sds((depth, width), BF16), (), 4 * depth * width, 4 * depth * width, 1)(directions)
 
     c1, s1, sums = call(
-        sums_kernel,
-        (sds((2 * rows, width), F32), sds((2 * rows, width), F32), sds((batch, 2 * KNOTS - 2, width), F32)),
+        functools.partial(sums_kernel, 2.0 * rows),
+        (sds((2 * rows, width), F32), sds((2 * rows, width), F32), sds((2 * KNOTS - 2, width), F32)),
         (pltpu.VMEM((2 * rows, width), F32), pltpu.VMEM((2 * KNOTS - 2, 8, width), F32)),
         4 * rows * depth * width,
         8 * rows * depth,
         3,
     )(mine, other, unit)
-    sums = lax.all_to_all(sums, "y", 0, 0, tiled=True)
-
-    def grad(*refs):
-        grad_kernel(total_rows, *refs)
+    sums = to_all(sums.astype(LINK), "y", batch).astype(F32)
 
     kept, theirs = call(
-        grad,
+        functools.partial(grad_kernel, total_rows),
         (sds((rows, width), BF16), sds((rows, depth), F32)),
         (pltpu.VMEM((2 * rows, width), BF16), pltpu.VMEM((2 * KNOTS, 8, width), F32)),
         2 * rows * depth * width,
         4 * rows * depth,
         4,
     )(c1, s1, sums, unit)
-    arrived = lax.ppermute(theirs, "c", swap)
+    arrived = turn(theirs, "c", 1)
     ours = call(times_unit, sds((rows, depth), F32), (), 2 * rows * depth * width, 4 * rows * depth, 2)(kept, unit)
-    part = (ours + arrived).astype(BF16).reshape(near, rows // near, depth)
-    part = lax.all_to_all(part, ("zl", "x"), 0, 0, tiled=True)
-    part = jnp.sum(part.astype(F32), axis=0).reshape(far, -1, depth)
-    part = lax.all_to_all(part, "zh", 0, 0, tiled=True)
-    return jnp.sum(part, axis=0)
+    parts = (ours + arrived).reshape(along_x, block, depth)
+    back = [turn(parts[j].astype(LINK), "x", by) for j, by in ((1, 2), (2, along_x - 1), (3, 1))]
+    part = parts[0] + sum(p.astype(F32) for p in back)
+    part = part.astype(LINK).reshape(ring, -1, depth)
+    part = lax.all_to_all(part, "z", 0, 0, tiled=True)
+    return jnp.sum(part.astype(F32), axis=0)
 
 
 def solution(mesh):
-    fine = Mesh(mesh.devices.reshape(8, 4, 3, 4, 2), ("y", "zh", "zl", "x", "c"))
-    along = ("zh", "zl", "x", "c")
+    fine = Mesh(mesh.devices.reshape(8, 12, 4, 2), ("y", "z", "x", "c"))
+    along = ("z", "x", "c")
     rows = P(("y",) + along, None)
     return jax.shard_map(local, mesh=fine, in_specs=(rows, P(None, along)), out_specs=rows, check_vma=False)

time: 115 us -> 110 us (0.957)
  blocking collectives: 98.7 us -> 62.4 us
  starting transfers between devices: 3.83 us -> 22.1 us
  waiting for transfers between devices: 4.85 us -> 17.2 us
    all_to_all x3 -> x1, blocking collectives: 54.7 us -> 17.3 us  [local(): part = lax.all_to_all(part, 'z', 0, 0, tiled=True)]
    ppermute x2 -> x8, starting transfers between devices: 3.83 us -> 22.1 us  [turn(): return lax.ppermute(x, axis, [(i, (i + by) % n) for i in range(n)])]
    ppermute x2 -> x8, waiting for transfers between devices: 4.85 us -> 17.2 us  [turn(): return lax.ppermute(x, axis, [(i, (i + by) % n) for i in range(n)])]
  transfers between devices with their start and end apart: 2 -> 8, of which waited for: 2 -> 6; matrix products, arithmetic and copies ran while one was open for 0% -> 0% of each run, Pallas kernels for 1% -> 1%
where the time goes in v2:
time: 110 us; the launch traced here: 109 us
  blocking collectives  62.4 us (57%)
  starting transfers between devices  22.1 us (20%)
  waiting for transfers between devices  17.2 us (16%)
  Pallas kernels  5.04 us (5%)
  other arithmetic  1.2 us (1%)
  local copies, waits for them, and re-layouts  1.18 us (1%)
    all_to_all x2, blocking collectives, to_all(): lax.all_to_all(jnp.broadcast_to(x[None], (peers,) + x.shape), axes, 0, 0,...  45.2 us
    ppermute x8, starting transfers between devices, turn(): return lax.ppermute(x, axis, [(i, (i + by) % n) for i in range(n)])  22.1 us
    all_to_all x1, blocking collectives, local(): part = lax.all_to_all(part, 'z', 0, 0, tiled=True)  17.3 us
    ppermute x8, waiting for transfers between devices, turn(): return lax.ppermute(x, axis, [(i, (i + by) % n) for i in range(n)])  17.2 us
    pallas_call x1, Pallas kernels, local(): call(functools.partial(sums_kernel, 2.0 * rows), (sds((2 * rows, width),...  2.37 us
  transfers between devices with their start and end apart: 8, of which 6 were waited for; matrix products, arithmetic and copies ran while one was open for 0% of the time, Pallas kernels for 1%

profile of v2, /device:TPU:6, one launch (start us, length us, event | category | flops | bytes accessed | tf_op | source)
XLA Modules:
  0.0 109.3 jit_solution(5474693921532528299)
XLA Ops:
  0.0 0.0 copy-start
  0.0 0.9 broadcast_in_dim.4
  0.9 28.9 %all_to_all.15 = bf16[12,4,2048]{2,1,0:T(4,128)(2,1)S(1)} all-to-all(bf16[12,4,2048]{2,1,0:T(4,128)(2,1)S(1)} %broadcast_in_dim.4), channel_id=1, replica_groups=mesh['y'=8,'z'=12,'x'=4,'c'=2] {'z'}, dimensions={0} | all-to-all | bytes 393216 | tf_op jit(solution)/shard_map/all_to_all | solution.py:138
  29.8 3.3 %collective-permute-start = (bf16[48,2048]{1,0:T(8,128)(2,1)S(1)}, bf16[48,2048]{1,0:T(8,128)(2,1)S(1)}, u32[]{:S(2)}, u32[]{:S(2)}) collective-permute-start(bf16[48,2048]{1,0:T(8,128)(2,1)S(1)} %reshape.17), channel_id=1, source_target_pairs={{0,4},{2,6},{4,0},{6,2},{1,5},{3,7},{5,1},{7,3},{8,12},{10,14},{12... | collective-permute-start | bytes 589832 | tf_op jit(solution)/shard_map/ppermute | solution.py:143
  33.2 4.0 %collective-permute-start.1 = (bf16[48,2048]{1,0:T(8,128)(2,1)S(1)}, bf16[48,2048]{1,0:T(8,128)(2,1)S(1)}, u32[]{:S(2)}, u32[]{:S(2)}) collective-permute-start(bf16[48,2048]{1,0:T(8,128)(2,1)S(1)} %reshape.17), channel_id=1, source_target_pairs={{0,2},{2,4},{4,6},{6,0},{1,3},{3,5},{5,7},{7,1},{8,10},{10,12},{12... | collective-permute-start | bytes 589832 | tf_op jit(solution)/shard_map/ppermute | solution.py:143
  37.2 1.9 %collective-permute-start.2 = (bf16[48,2048]{1,0:T(8,128)(2,1)S(1)}, bf16[48,2048]{1,0:T(8,128)(2,1)S(1)}, u32[]{:S(2)}, u32[]{:S(2)}) collective-permute-start(bf16[48,2048]{1,0:T(8,128)(2,1)S(1)} %reshape.17), channel_id=1, source_target_pairs={{0,6},{2,0},{4,2},{6,4},{1,7},{3,1},{5,3},{7,5},{8,14},{10,8},{12,... | collective-permute-start | bytes 589832 | tf_op jit(solution)/shard_map/ppermute | solution.py:143
  39.1 0.0 collective-permute-done
  39.2 1.8 %collective-permute-done.1 = bf16[48,2048]{1,0:T(8,128)(2,1)S(1)} collective-permute-done((bf16[48,2048]{1,0:T(8,128)(2,1)S(1)}, bf16[48,2048]{1,0:T(8,128)(2,1)S(1)}, u32[]{:S(2)}, u32[]{:S(2)}) %collective-permute-start.1) | collective-permute-done | bytes 196640 | tf_op jit(solution)/shard_map/ppermute | solution.py:143
  41.0 5.0 %collective-permute-done.2 = bf16[48,2048]{1,0:T(8,128)(2,1)S(1)} collective-permute-done((bf16[48,2048]{1,0:T(8,128)(2,1)S(1)}, bf16[48,2048]{1,0:T(8,128)(2,1)S(1)}, u32[]{:S(2)}, u32[]{:S(2)}) %collective-permute-start.2) | collective-permute-done | bytes 196640 | tf_op jit(solution)/shard_map/ppermute | solution.py:143
  46.0 1.9 %collective-permute-start.3 = (bf16[192,2048]{1,0:T(8,128)(2,1)S(1)}, bf16[192,2048]{1,0:T(8,128)(2,1)S(1)}, u32[]{:S(2)}, u32[]{:S(2)}) collective-permute-start(bf16[192,2048]{1,0:T(8,128)(2,1)S(1)} %constant_dynamic-update-slice_fusion.mine_ref), channel_id=1, source_target_pairs={{0,1},{1,0},{2,3},{3,2},{4,5},{5,4},{6,7},{7,6},{8,9},{9,8},{10,11... | collective-permute-start | bytes 2359304 | tf_op jit(solution)/shard_map/ppermute | solution.py:143
  47.9 0.0 copy-done
  47.9 0.3 shard_map.28.unit_ref
  48.2 2.0 %collective-permute-done.3.other_ref = bf16[192,2048]{1,0:T(8,128)(2,1)S(1)} collective-permute-done((bf16[192,2048]{1,0:T(8,128)(2,1)S(1)}, bf16[192,2048]{1,0:T(8,128)(2,1)S(1)}, u32[]{:S(2)}, u32[]{:S(2)}) %collective-permute-start.3) | collective-permute-done | bytes 786464 | tf_op jit(solution)/shard_map/ppermute | solution.py:143
  50.2 2.4 %shard_map.29 = (f32[384,256]{1,0:T(8,128)S(1)}, f32[384,256]{1,0:T(8,128)S(1)}, f32[32,256]{1,0:T(8,128)S(1)}) custom-call(bf16[192,2048]{1,0:T(8,128)(2,1)S(1)} %constant_dynamic-update-slice_fusion.mine_ref, bf16[192,2048]{1,0:T(8,128)(2,1)S(1)} %collective-permute-done.3.other_ref, bf16[2048,256]{1,0:T(8,128)(2,1)S(1)} %shard_map.28.unit_ref), custom_call_target="tpu_custom_call" | custom-call | flops 402653184 | bytes 3145728 | tf_op jit(solution)/shard_map/pallas_call | solution.py:160
  52.6 16.3 %all_to_all.16 = f16[8,32,256]{2,1,0:T(8,128)(2,1)S(1)} all-to-all(f16[8,32,256]{2,1,0:T(8,128)(2,1)S(1)} %broadcast_in_dim.5), channel_id=1, replica_groups=mesh['y'=8,'z'=12,'x'=4,'c'=2] {'y'}, dimensions={0} | all-to-all | bytes 262144 | tf_op jit(solution)/shard_map/all_to_all | solution.py:138
  68.9 1.9 %shard_map.30 = (bf16[192,256]{1,0:T(8,128)(2,1)S(1)}, f32[192,2048]{1,0:T(8,128)S(1)}) custom-call(f32[384,256]{1,0:T(8,128)S(1)} %get-tuple-element.10.c_ref, f32[384,256]{1,0:T(8,128)S(1)} %get-tuple-element.11.s_ref, f32[8,32,256]{2,1,0:T(8,128)S(1)} %convert_element_type.25.sums_ref, bf16[2048,256]{1,0:T(8,128)(2,1)S(1)} %shard_map.28.unit_ref), custom_call_target="tpu_custom_call" | custom-call | flops 201326592 | bytes 1572864 | tf_op jit(solution)/shard_map/pallas_call | solution.py:170
  70.8 1.9 %collective-permute-start.4 = (f32[192,2048]{1,0:T(8,128)S(1)}, f32[192,2048]{1,0:T(8,128)S(1)}, u32[]{:S(2)}, u32[]{:S(2)}) collective-permute-start(f32[192,2048]{1,0:T(8,128)S(1)} %get-tuple-element.14), channel_id=1, source_target_pairs={{0,1},{1,0},{2,3},{3,2},{4,5},{5,4},{6,7},{7,6},{8,9},{9,8},{10,11... | collective-permute-start | bytes 4718600 | tf_op jit(solution)/shard_map/ppermute | solution.py:143
  72.7 0.5 shard_map.31
  73.2 2.9 %collective-permute-done.4 = f32[192,2048]{1,0:T(8,128)S(1)} collective-permute-done((f32[192,2048]{1,0:T(8,128)S(1)}, f32[192,2048]{1,0:T(8,128)S(1)}, u32[]{:S(2)}, u32[]{:S(2)}) %collective-permute-start.4) | collective-permute-done | bytes 1572896 | tf_op jit(solution)/shard_map/ppermute | solution.py:143
  76.1 0.3 fusion.1
  76.4 0.1 fusion.2
  76.5 1.9 %collective-permute-start.5 = (f16[48,2048]{1,0:T(8,128)(2,1)S(1)}, f16[48,2048]{1,0:T(8,128)(2,1)S(1)}, u32[]{:S(2)}, u32[]{:S(2)}) collective-permute-start(f16[48,2048]{1,0:T(8,128)(2,1)S(1)} %get-tuple-element.17), channel_id=1, source_target_pairs={{0,4},{2,6},{4,0},{6,2},{1,5},{3,7},{5,1},{7,3},{8,12},{10,14},{12... | collective-permute-start | bytes 589832 | tf_op jit(solution)/shard_map/ppermute | solution.py:143
  78.5 2.3 %collective-permute-start.6 = (f16[48,2048]{1,0:T(8,128)(2,1)S(1)}, f16[48,2048]{1,0:T(8,128)(2,1)S(1)}, u32[]{:S(2)}, u32[]{:S(2)}) collective-permute-start(f16[48,2048]{1,0:T(8,128)(2,1)S(1)} %get-tuple-element.19), channel_id=1, source_target_pairs={{0,6},{2,0},{4,2},{6,4},{1,7},{3,1},{5,3},{7,5},{8,14},{10,8},{12,... | collective-permute-start | bytes 589832 | tf_op jit(solution)/shard_map/ppermute | solution.py:143
  80.8 4.8 %collective-permute-start.7 = (f16[48,2048]{1,0:T(8,128)(2,1)S(1)}, f16[48,2048]{1,0:T(8,128)(2,1)S(1)}, u32[]{:S(2)}, u32[]{:S(2)}) collective-permute-start(f16[48,2048]{1,0:T(8,128)(2,1)S(1)} %get-tuple-element.18), channel_id=1, source_target_pairs={{0,2},{2,4},{4,6},{6,0},{1,3},{3,5},{5,7},{7,1},{8,10},{10,12},{12... | collective-permute-start | bytes 589832 | tf_op jit(solution)/shard_map/ppermute | solution.py:143
  85.5 2.2 %collective-permute-done.5 = f16[48,2048]{1,0:T(8,128)(2,1)S(1)} collective-permute-done((f16[48,2048]{1,0:T(8,128)(2,1)S(1)}, f16[48,2048]{1,0:T(8,128)(2,1)S(1)}, u32[]{:S(2)}, u32[]{:S(2)}) %collective-permute-start.5) | collective-permute-done | bytes 196640 | tf_op jit(solution)/shard_map/ppermute | solution.py:143
  87.7 3.4 %collective-permute-done.6 = f16[48,2048]{1,0:T(8,128)(2,1)S(1)} collective-permute-done((f16[48,2048]{1,0:T(8,128)(2,1)S(1)}, f16[48,2048]{1,0:T(8,128)(2,1)S(1)}, u32[]{:S(2)}, u32[]{:S(2)}) %collective-permute-start.6) | collective-permute-done | bytes 196640 | tf_op jit(solution)/shard_map/ppermute | solution.py:143
  91.1 0.0 collective-permute-done.7
  91.1 0.1 fusion
  91.2 0.1 reshape.18
  91.3 17.3 %all_to_all.17 = f16[12,4,2048]{2,1,0:T(4,128)(2,1)S(1)} all-to-all(f16[12,4,2048]{2,1,0:T(4,128)(2,1)S(1)} %reshape.18), channel_id=1, replica_groups=mesh['y'=8,'z'=12,'x'=4,'c'=2] {'z'}, dimensions={0} | all-to-all | bytes 393216 | tf_op jit(solution)/shard_map/all_to_all | solution.py:184
  108.6 0.7 convert_reduce_fusion
  (8 shorter events, 0.1 us)
Async XLA Ops:
  0.0 47.9 %copy-start = (bf16[2048,256]{1,0:T(8,128)(2,1)S(1)}, bf16[2048,256]{1,0:T(8,128)(2,1)}, u32[]{:S(2)}) copy-start(bf16[2048,256]{1,0:T(8,128)(2,1)} %dir_ref.1) | copy-start | bytes 3145732
  29.8 9.3 %collective-permute-start = (bf16[48,2048]{1,0:T(8,128)(2,1)S(1)}, bf16[48,2048]{1,0:T(8,128)(2,1)S(1)}, u32[]{:S(2)}, u32[]{:S(2)}) collective-permute-start(bf16[48,2048]{1,0:T(8,128)(2,1)S(1)} %reshape.17), channel_id=1, source_target_pairs={{0,4},{2,6},{4,0},{6,2},{1,5},{3,7},{5,1},{7,3},{8,12},{10,14},{12... | collective-permute-start | bytes 589832 | tf_op jit(solution)/shard_map/ppermute | solution.py:143
  33.2 7.8 %collective-permute-start.1 = (bf16[48,2048]{1,0:T(8,128)(2,1)S(1)}, bf16[48,2048]{1,0:T(8,128)(2,1)S(1)}, u32[]{:S(2)}, u32[]{:S(2)}) collective-permute-start(bf16[48,2048]{1,0:T(8,128)(2,1)S(1)} %reshape.17), channel_id=1, source_target_pairs={{0,2},{2,4},{4,6},{6,0},{1,3},{3,5},{5,7},{7,1},{8,10},{10,12},{12... | collective-permute-start | bytes 589832 | tf_op jit(solution)/shard_map/ppermute | solution.py:143
  37.2 8.8 %collective-permute-start.2 = (bf16[48,2048]{1,0:T(8,128)(2,1)S(1)}, bf16[48,2048]{1,0:T(8,128)(2,1)S(1)}, u32[]{:S(2)}, u32[]{:S(2)}) collective-permute-start(bf16[48,2048]{1,0:T(8,128)(2,1)S(1)} %reshape.17), channel_id=1, source_target_pairs={{0,6},{2,0},{4,2},{6,4},{1,7},{3,1},{5,3},{7,5},{8,14},{10,8},{12,... | collective-permute-start | bytes 589832 | tf_op jit(solution)/shard_map/ppermute | solution.py:143
  46.0 4.2 %collective-permute-start.3 = (bf16[192,2048]{1,0:T(8,128)(2,1)S(1)}, bf16[192,2048]{1,0:T(8,128)(2,1)S(1)}, u32[]{:S(2)}, u32[]{:S(2)}) collective-permute-start(bf16[192,2048]{1,0:T(8,128)(2,1)S(1)} %constant_dynamic-update-slice_fusion.mine_ref), channel_id=1, source_target_pairs={{0,1},{1,0},{2,3},{3,2},{4,5},{5,4},{6,7},{7,6},{8,9},{9,8},{10,11... | collective-permute-start | bytes 2359304 | tf_op jit(solution)/shard_map/ppermute | solution.py:143
  70.8 5.3 %collective-permute-start.4 = (f32[192,2048]{1,0:T(8,128)S(1)}, f32[192,2048]{1,0:T(8,128)S(1)}, u32[]{:S(2)}, u32[]{:S(2)}) collective-permute-start(f32[192,2048]{1,0:T(8,128)S(1)} %get-tuple-element.14), channel_id=1, source_target_pairs={{0,1},{1,0},{2,3},{3,2},{4,5},{5,4},{6,7},{7,6},{8,9},{9,8},{10,11... | collective-permute-start | bytes 4718600 | tf_op jit(solution)/shard_map/ppermute | solution.py:143
  76.5 11.2 %collective-permute-start.5 = (f16[48,2048]{1,0:T(8,128)(2,1)S(1)}, f16[48,2048]{1,0:T(8,128)(2,1)S(1)}, u32[]{:S(2)}, u32[]{:S(2)}) collective-permute-start(f16[48,2048]{1,0:T(8,128)(2,1)S(1)} %get-tuple-element.17), channel_id=1, source_target_pairs={{0,4},{2,6},{4,0},{6,2},{1,5},{3,7},{5,1},{7,3},{8,12},{10,14},{12... | collective-permute-start | bytes 589832 | tf_op jit(solution)/shard_map/ppermute | solution.py:143
  78.5 12.6 %collective-permute-start.6 = (f16[48,2048]{1,0:T(8,128)(2,1)S(1)}, f16[48,2048]{1,0:T(8,128)(2,1)S(1)}, u32[]{:S(2)}, u32[]{:S(2)}) collective-permute-start(f16[48,2048]{1,0:T(8,128)(2,1)S(1)} %get-tuple-element.19), channel_id=1, source_target_pairs={{0,6},{2,0},{4,2},{6,4},{1,7},{3,1},{5,3},{7,5},{8,14},{10,8},{12,... | collective-permute-start | bytes 589832 | tf_op jit(solution)/shard_map/ppermute | solution.py:143
  80.8 10.3 %collective-permute-start.7 = (f16[48,2048]{1,0:T(8,128)(2,1)S(1)}, f16[48,2048]{1,0:T(8,128)(2,1)S(1)}, u32[]{:S(2)}, u32[]{:S(2)}) collective-permute-start(f16[48,2048]{1,0:T(8,128)(2,1)S(1)} %get-tuple-element.18), channel_id=1, source_target_pairs={{0,2},{2,4},{4,6},{6,0},{1,3},{3,5},{5,7},{7,1},{8,10},{10,12},{12... | collective-permute-start | bytes 589832 | tf_op jit(solution)/shard_map/ppermute | solution.py:143

commit v3 on v2

--- a/solution.py
+++ b/solution.py
@@ -45,11 +45,11 @@
         unit_ref[pl.ds(i * rows, rows), :] = (w * inv).astype(BF16)
 
 
-def sums_kernel(local_rows, mine_ref, other_ref, unit_ref, c_ref, s_ref, out_ref, proj_ref, acc_ref):
-    half = mine_ref.shape[0]
+def sums_kernel(rows_ref, unit_ref, more_ref, c_ref, s_ref, out_ref, proj_ref, acc_ref):
     rows, width = proj_ref.shape
-    proj_ref[pl.ds(0, half), :] = jnp.dot(mine_ref[...], unit_ref[...], preferred_element_type=F32)
-    proj_ref[pl.ds(half, half), :] = jnp.dot(other_ref[...], unit_ref[...], preferred_element_type=F32)
+    half = width // 2
+    proj_ref[:, pl.ds(0, half)] = jnp.dot(rows_ref[...], unit_ref[...], preferred_element_type=F32)
+    proj_ref[:, pl.ds(half, half)] = jnp.dot(rows_ref[...], more_ref[...], preferred_element_type=F32)
     acc_ref[...] = jnp.zeros_like(acc_ref)
 
     def fold(v):
@@ -73,12 +73,11 @@
 
     out_ref[...] = jnp.sum(acc_ref[...], axis=1)
     for k in range(1, KNOTS):
-        out_ref[pl.ds(k - 1, 1), :] -= local_rows * TARGET[k]
+        out_ref[pl.ds(k - 1, 1), :] -= rows * TARGET[k]
 
 
-def grad_kernel(total_rows, c_ref, s_ref, sums_ref, unit_ref, mine_ref, out_ref, g_ref, rep_ref):
+def grad_kernel(total_rows, c_ref, s_ref, sums_ref, unit_ref, more_ref, out_ref, g_ref, rep_ref):
     rows, width = c_ref.shape
-    half = rows // 2
     sums = jnp.sum(sums_ref[...], axis=0)
     for k in range(KNOTS):
         if k == 0:
@@ -108,17 +107,16 @@
         g = rep_ref[0] + (c1 * a1 - a2) + s1 * b1
         g_ref[at, :] = g.reshape(TILE, width).astype(BF16)
 
-    mine_ref[...] = g_ref[pl.ds(0, half), :]
-    times_unit(g_ref.at[pl.ds(half, half), :], unit_ref, out_ref)
+    step, half = 512, width // 2
+    for j in range(unit_ref.shape[0] // step):
+        at = pl.ds(j * step, step)
+        out_ref[:, at] = times_transposed(g_ref[:, pl.ds(0, half)], unit_ref[at, :]) + times_transposed(
+            g_ref[:, pl.ds(half, half)], more_ref[at, :]
+        )
 
 
-def times_unit(g_ref, unit_ref, out_ref):
-    step = 512
-    for j in range(unit_ref.shape[0] // step):
-        at = pl.ds(j * step, step)
-        out_ref[:, at] = lax.dot_general(
-            g_ref[...], unit_ref[at, :], (((1,), (1,)), ((), ())), preferred_element_type=F32
-        )
+def times_transposed(a, b):
+    return lax.dot_general(a, b, (((1,), (1,)), ((), ())), preferred_element_type=F32)
 
 
 def call(kernel, outs, scratch, flops, moved, operands):
@@ -153,31 +151,33 @@
 
     held = to_all(embeddings, "z", ring).reshape(block, depth)
     far = [turn(held, "x", by) for by in (2, 1, along_x - 1)]
-    mine = jnp.concatenate([held] + far, axis=0)
-    other = turn(mine, "c", 1)
-    unit = call(unit_kernel, sds((depth, width), BF16), (), 4 * depth * width, 4 * depth * width, 1)(directions)
+    directions, anchor = lax.optimization_barrier((directions, held))
+    units = [
+        call(unit_kernel, sds((depth, width), BF16), (), 4 * depth * width, 4 * depth * width, 1)(d)
+        for d in (directions, turn(directions, "c", 1))
+    ]
+    mine = jnp.concatenate([anchor] + far, axis=0)
 
     c1, s1, sums = call(
-        functools.partial(sums_kernel, 2.0 * rows),
-        (sds((2 * rows, width), F32), sds((2 * rows, width), F32), sds((2 * KNOTS - 2, width), F32)),
-        (pltpu.VMEM((2 * rows, width), F32), pltpu.VMEM((2 * KNOTS - 2, 8, width), F32)),
+        sums_kernel,
+        (sds((rows, 2 * width), F32), sds((rows, 2 * width), F32), sds((2 * KNOTS - 2, 2 * width), F32)),
+        (pltpu.VMEM((rows, 2 * width), F32), pltpu.VMEM((2 * KNOTS - 2, 8, 2 * width), F32)),
         4 * rows * depth * width,
         8 * rows * depth,
         3,
-    )(mine, other, unit)
+    )(mine, *units)
+    swapped = turn(sums, "c", 1)
+    sums = sums + jnp.concatenate([swapped[:, width:], swapped[:, :width]], axis=1)
     sums = to_all(sums.astype(LINK), "y", batch).astype(F32)
 
-    kept, theirs = call(
+    parts = call(
         functools.partial(grad_kernel, total_rows),
-        (sds((rows, width), BF16), sds((rows, depth), F32)),
-        (pltpu.VMEM((2 * rows, width), BF16), pltpu.VMEM((2 * KNOTS, 8, width), F32)),
-        2 * rows * depth * width,
+        sds((rows, depth), F32),
+        (pltpu.VMEM((rows, 2 * width), BF16), pltpu.VMEM((2 * KNOTS, 8, 2 * width), F32)),
+        4 * rows * depth * width,
         4 * rows * depth,
-        4,
-    )(c1, s1, sums, unit)
-    arrived = turn(theirs, "c", 1)
-    ours = call(times_unit, sds((rows, depth), F32), (), 2 * rows * depth * width, 4 * rows * depth, 2)(kept, unit)
-    parts = (ours + arrived).reshape(along_x, block, depth)
+        5,
+    )(c1, s1, sums, *units).reshape(along_x, block, depth)
     back = [turn(parts[j].astype(LINK), "x", by) for j, by in ((1, 2), (2, along_x - 1), (3, 1))]
     part = parts[0] + sum(p.astype(F32) for p in back)
     part = part.astype(LINK).reshape(ring, -1, depth)

time: 110 us -> 109 us (level)
  waiting for transfers between devices: 17.2 us -> 14.3 us
  local copies, waits for them, and re-layouts: 1.18 us -> 2.3 us
    ppermute x8, waiting for transfers between devices: 17.2 us -> 14.3 us  [turn(): return lax.ppermute(x, axis, [(i, (i + by) % n) for i in range(n)])]
    all_to_all x2, blocking collectives: 45.2 us -> 48 us  [to_all(): lax.all_to_all(jnp.broadcast_to(x[None], (peers,) + x.shape), axes, 0, 0,...]
    all_to_all x1, blocking collectives: 17.3 us -> 15.3 us  [local(): part = lax.all_to_all(part, 'z', 0, 0, tiled=True)]
    unnamed x5 -> x2, local copies, waits for them, and re-layouts: 0.05 us -> 1.22 us
    pallas_call x3 -> x2, Pallas kernels: 4.78 us -> 4.72 us  [the longest x1 2.53 us: local(): call(sums_kernel, (sds((rows, 2 * width), F32), sds((rows, 2 * width), F3...]
  transfers between devices with their start and end apart: 8 -> 8, of which waited for: 6 -> 6; matrix products, arithmetic and copies ran while one was open for 0% -> 0% of each run, Pallas kernels for 1% -> 0%
where the time goes in v3:
time: 109 us; the launch traced here: 108 us
  blocking collectives  63.4 us (58%)
  starting transfers between devices  21.9 us (20%)
  waiting for transfers between devices  14.3 us (13%)
  Pallas kernels  5.24 us (5%)
  local copies, waits for them, and re-layouts  2.3 us (2%)
    all_to_all x2, blocking collectives, to_all(): lax.all_to_all(jnp.broadcast_to(x[None], (peers,) + x.shape), axes, 0, 0,...  48 us
    ppermute x8, starting transfers between devices, turn(): return lax.ppermute(x, axis, [(i, (i + by) % n) for i in range(n)])  21.9 us
    all_to_all x1, blocking collectives, local(): part = lax.all_to_all(part, 'z', 0, 0, tiled=True)  15.3 us
    ppermute x8, waiting for transfers between devices, turn(): return lax.ppermute(x, axis, [(i, (i + by) % n) for i in range(n)])  14.3 us
    pallas_call x1, Pallas kernels, local(): call(sums_kernel, (sds((rows, 2 * width), F32), sds((rows, 2 * width), F3...  2.53 us
    pallas_call x1, Pallas kernels, local(): call(functools.partial(grad_kernel, total_rows), sds((rows, depth), F32),...  2.19 us
  transfers between devices with their start and end apart: 8, of which 6 were waited for; matrix products, arithmetic and copies ran while one was open for 0% of the time, Pallas kernels for 0%

profile of v3, /device:TPU:6, one launch (start us, length us, event | category | flops | bytes accessed | tf_op | source)
XLA Modules:
  0.0 108.3 jit_solution(6455572509182472654)
XLA Ops:
  0.0 0.8 broadcast_in_dim.4
  0.8 28.9 %all_to_all.15 = bf16[12,4,2048]{2,1,0:T(4,128)(2,1)S(1)} all-to-all(bf16[12,4,2048]{2,1,0:T(4,128)(2,1)S(1)} %broadcast_in_dim.4), channel_id=1, replica_groups=mesh['y'=8,'z'=12,'x'=4,'c'=2] {'z'}, dimensions={0} | all-to-all | bytes 393216 | tf_op jit(solution)/shard_map/all_to_all | solution.py:136
  29.8 1.9 %collective-permute-start.3 = (bf16[2048,256]{1,0:T(8,128)(2,1)}, bf16[2048,256]{1,0:T(8,128)(2,1)S(1)}, u32[]{:S(2)}, u32[]{:S(2)}) collective-permute-start(bf16[2048,256]{1,0:T(8,128)(2,1)} %dir_ref), channel_id=1, source_target_pairs={{0,1},{1,0},{2,3},{3,2},{4,5},{5,4},{6,7},{7,6},{8,9},{9,8},{10,11... | collective-permute-start | bytes 3145736 | tf_op jit(solution)/shard_map/ppermute | solution.py:141
  31.7 2.7 %collective-permute-start.2 = (bf16[48,2048]{1,0:T(8,128)(2,1)S(1)}, bf16[48,2048]{1,0:T(8,128)(2,1)S(1)}, u32[]{:S(2)}, u32[]{:S(2)}) collective-permute-start(bf16[48,2048]{1,0:T(8,128)(2,1)S(1)} %reshape.17), channel_id=1, source_target_pairs={{0,6},{2,0},{4,2},{6,4},{1,7},{3,1},{5,3},{7,5},{8,14},{10,8},{12,... | collective-permute-start | bytes 589832 | tf_op jit(solution)/shard_map/ppermute | solution.py:141
  34.4 4.3 %collective-permute-start.1 = (bf16[48,2048]{1,0:T(8,128)(2,1)S(1)}, bf16[48,2048]{1,0:T(8,128)(2,1)S(1)}, u32[]{:S(2)}, u32[]{:S(2)}) collective-permute-start(bf16[48,2048]{1,0:T(8,128)(2,1)S(1)} %reshape.17), channel_id=1, source_target_pairs={{0,2},{2,4},{4,6},{6,0},{1,3},{3,5},{5,7},{7,1},{8,10},{10,12},{12... | collective-permute-start | bytes 589832 | tf_op jit(solution)/shard_map/ppermute | solution.py:141
  38.8 2.1 %collective-permute-start = (bf16[48,2048]{1,0:T(8,128)(2,1)S(1)}, bf16[48,2048]{1,0:T(8,128)(2,1)S(1)}, u32[]{:S(2)}, u32[]{:S(2)}) collective-permute-start(bf16[48,2048]{1,0:T(8,128)(2,1)S(1)} %reshape.17), channel_id=1, source_target_pairs={{0,4},{2,6},{4,0},{6,2},{1,5},{3,7},{5,1},{7,3},{8,12},{10,14},{12... | collective-permute-start | bytes 589832 | tf_op jit(solution)/shard_map/ppermute | solution.py:141
  40.9 0.0 copy-start
  40.9 1.2 %copy-done = bf16[2048,256]{1,0:T(8,128)(2,1)S(1)} copy-done((bf16[2048,256]{1,0:T(8,128)(2,1)S(1)}, bf16[2048,256]{1,0:T(8,128)(2,1)}, u32[]{:S(2)}) %copy-start) | copy-done | bytes 1048600
  42.1 0.3 shard_map.28.unit_ref
  42.4 0.0 collective-permute-done.2
  42.4 5.2 %collective-permute-done.1 = bf16[48,2048]{1,0:T(8,128)(2,1)S(1)} collective-permute-done((bf16[48,2048]{1,0:T(8,128)(2,1)S(1)}, bf16[48,2048]{1,0:T(8,128)(2,1)S(1)}, u32[]{:S(2)}, u32[]{:S(2)}) %collective-permute-start.1) | collective-permute-done | bytes 196640 | tf_op jit(solution)/shard_map/ppermute | solution.py:141
  47.5 1.4 %collective-permute-done = bf16[48,2048]{1,0:T(8,128)(2,1)S(1)} collective-permute-done((bf16[48,2048]{1,0:T(8,128)(2,1)S(1)}, bf16[48,2048]{1,0:T(8,128)(2,1)S(1)}, u32[]{:S(2)}, u32[]{:S(2)}) %collective-permute-start) | collective-permute-done | bytes 196640 | tf_op jit(solution)/shard_map/ppermute | solution.py:141
  48.9 0.1 pad_maximum_fusion.rows_ref
  49.0 0.0 collective-permute-done.3.dir_ref
  49.0 0.3 shard_map.29.more_ref
  49.2 2.5 %shard_map.30 = (f32[192,512]{1,0:T(8,128)S(1)}, f32[192,512]{1,0:T(8,128)S(1)}, f32[32,512]{1,0:T(8,128)S(1)}) custom-call(bf16[192,2048]{1,0:T(8,128)(2,1)S(1)} %pad_maximum_fusion.rows_ref, bf16[2048,256]{1,0:T(8,128)(2,1)S(1)} %shard_map.28.unit_ref, bf16[2048,256]{1,0:T(8,128)(2,1)S(1)} %shard_map.29.more_ref), custom_call_target="tpu_custom_call" | custom-call | flops 402653184 | bytes 3145728 | tf_op jit(solution)/shard_map/pallas_call | solution.py:161
  51.8 1.9 %collective-permute-start.4 = (f32[32,512]{1,0:T(8,128)S(1)}, f32[32,512]{1,0:T(8,128)S(1)}, u32[]{:S(2)}, u32[]{:S(2)}) collective-permute-start(f32[32,512]{1,0:T(8,128)S(1)} %get-tuple-element.14), channel_id=1, source_target_pairs={{0,1},{1,0},{2,3},{3,2},{4,5},{5,4},{6,7},{7,6},{8,9},{9,8},{10,11... | collective-permute-start | bytes 196616 | tf_op jit(solution)/shard_map/ppermute | solution.py:141
  53.7 1.2 %collective-permute-done.4 = f32[32,512]{1,0:T(8,128)S(1)} collective-permute-done((f32[32,512]{1,0:T(8,128)S(1)}, f32[32,512]{1,0:T(8,128)S(1)}, u32[]{:S(2)}, u32[]{:S(2)}) %collective-permute-start.4) | collective-permute-done | bytes 65568 | tf_op jit(solution)/shard_map/ppermute | solution.py:141
  55.0 19.1 %all_to_all.16 = f16[8,32,512]{2,1,0:T(8,128)(2,1)S(1)} all-to-all(f16[8,32,512]{2,1,0:T(8,128)(2,1)S(1)} %broadcast_in_dim.5), channel_id=1, replica_groups=mesh['y'=8,'z'=12,'x'=4,'c'=2] {'y'}, dimensions={0} | all-to-all | bytes 524288 | tf_op jit(solution)/shard_map/all_to_all | solution.py:136
  74.1 0.1 convert_element_type.25.sums_ref
  74.1 2.2 %shard_map.31 = f32[192,2048]{1,0:T(8,128)S(1)} custom-call(f32[192,512]{1,0:T(8,128)S(1)} %get-tuple-element.12.c_ref, f32[192,512]{1,0:T(8,128)S(1)} %get-tuple-element.13.s_ref, f32[8,32,512]{2,1,0:T(8,128)S(1)} %convert_element_type.25.sums_ref, bf16[2048,256]{1,0:T(8,128)(2,1)S(1)} %shard_map.28.unit_ref, bf16[2048,256]{1,0:T(8,128)(2,1)S(1)} %shard_map.29.more_ref), custom_call_target="tpu_custom_call" | custom-call | flops 402653184 | bytes 1572864 | tf_op jit(solution)/shard_map/pallas_call | solution.py:173
  76.3 0.1 convert.5
  76.5 0.1 fusion.2
  76.6 2.2 %collective-permute-start.5 = (f16[48,2048]{1,0:T(8,128)(2,1)S(1)}, f16[48,2048]{1,0:T(8,128)(2,1)S(1)}, u32[]{:S(2)}, u32[]{:S(2)}) collective-permute-start(f16[48,2048]{1,0:T(8,128)(2,1)S(1)} %get-tuple-element.15), channel_id=1, source_target_pairs={{0,4},{2,6},{4,0},{6,2},{1,5},{3,7},{5,1},{7,3},{8,12},{10,14},{12... | collective-permute-start | bytes 589832 | tf_op jit(solution)/shard_map/ppermute | solution.py:141
  78.8 4.5 %collective-permute-start.7 = (f16[48,2048]{1,0:T(8,128)(2,1)S(1)}, f16[48,2048]{1,0:T(8,128)(2,1)S(1)}, u32[]{:S(2)}, u32[]{:S(2)}) collective-permute-start(f16[48,2048]{1,0:T(8,128)(2,1)S(1)} %get-tuple-element.16), channel_id=1, source_target_pairs={{0,2},{2,4},{4,6},{6,0},{1,3},{3,5},{5,7},{7,1},{8,10},{10,12},{12... | collective-permute-start | bytes 589832 | tf_op jit(solution)/shard_map/ppermute | solution.py:141
  83.3 2.2 %collective-permute-start.6 = (f16[48,2048]{1,0:T(8,128)(2,1)S(1)}, f16[48,2048]{1,0:T(8,128)(2,1)S(1)}, u32[]{:S(2)}, u32[]{:S(2)}) collective-permute-start(f16[48,2048]{1,0:T(8,128)(2,1)S(1)} %get-tuple-element.17), channel_id=1, source_target_pairs={{0,6},{2,0},{4,2},{6,4},{1,7},{3,1},{5,3},{7,5},{8,14},{10,8},{12,... | collective-permute-start | bytes 589832 | tf_op jit(solution)/shard_map/ppermute | solution.py:141
  85.5 0.2 collective-permute-done.5
  85.7 3.8 %collective-permute-done.7 = f16[48,2048]{1,0:T(8,128)(2,1)S(1)} collective-permute-done((f16[48,2048]{1,0:T(8,128)(2,1)S(1)}, f16[48,2048]{1,0:T(8,128)(2,1)S(1)}, u32[]{:S(2)}, u32[]{:S(2)}) %collective-permute-start.7) | collective-permute-done | bytes 196640 | tf_op jit(solution)/shard_map/ppermute | solution.py:141
  89.5 2.6 %collective-permute-done.6 = f16[48,2048]{1,0:T(8,128)(2,1)S(1)} collective-permute-done((f16[48,2048]{1,0:T(8,128)(2,1)S(1)}, f16[48,2048]{1,0:T(8,128)(2,1)S(1)}, u32[]{:S(2)}, u32[]{:S(2)}) %collective-permute-start.6) | collective-permute-done | bytes 196640 | tf_op jit(solution)/shard_map/ppermute | solution.py:141
  92.1 0.1 fusion
  92.2 0.1 reshape.18
  92.3 15.3 %all_to_all.17 = f16[12,4,2048]{2,1,0:T(4,128)(2,1)S(1)} all-to-all(f16[12,4,2048]{2,1,0:T(4,128)(2,1)S(1)} %reshape.18), channel_id=1, replica_groups=mesh['y'=8,'z'=12,'x'=4,'c'=2] {'z'}, dimensions={0} | all-to-all | bytes 393216 | tf_op jit(solution)/shard_map/all_to_all | solution.py:184
  107.6 0.7 convert_reduce_fusion
  (4 shorter events, 0.1 us)
Async XLA Ops:
  29.8 19.2 %collective-permute-start.3 = (bf16[2048,256]{1,0:T(8,128)(2,1)}, bf16[2048,256]{1,0:T(8,128)(2,1)S(1)}, u32[]{:S(2)}, u32[]{:S(2)}) collective-permute-start(bf16[2048,256]{1,0:T(8,128)(2,1)} %dir_ref), channel_id=1, source_target_pairs={{0,1},{1,0},{2,3},{3,2},{4,5},{5,4},{6,7},{7,6},{8,9},{9,8},{10,11... | collective-permute-start | bytes 3145736 | tf_op jit(solution)/shard_map/ppermute | solution.py:141
  31.7 10.7 %collective-permute-start.2 = (bf16[48,2048]{1,0:T(8,128)(2,1)S(1)}, bf16[48,2048]{1,0:T(8,128)(2,1)S(1)}, u32[]{:S(2)}, u32[]{:S(2)}) collective-permute-start(bf16[48,2048]{1,0:T(8,128)(2,1)S(1)} %reshape.17), channel_id=1, source_target_pairs={{0,6},{2,0},{4,2},{6,4},{1,7},{3,1},{5,3},{7,5},{8,14},{10,8},{12,... | collective-permute-start | bytes 589832 | tf_op jit(solution)/shard_map/ppermute | solution.py:141
  34.4 13.1 %collective-permute-start.1 = (bf16[48,2048]{1,0:T(8,128)(2,1)S(1)}, bf16[48,2048]{1,0:T(8,128)(2,1)S(1)}, u32[]{:S(2)}, u32[]{:S(2)}) collective-permute-start(bf16[48,2048]{1,0:T(8,128)(2,1)S(1)} %reshape.17), channel_id=1, source_target_pairs={{0,2},{2,4},{4,6},{6,0},{1,3},{3,5},{5,7},{7,1},{8,10},{10,12},{12... | collective-permute-start | bytes 589832 | tf_op jit(solution)/shard_map/ppermute | solution.py:141
  38.8 10.1 %collective-permute-start = (bf16[48,2048]{1,0:T(8,128)(2,1)S(1)}, bf16[48,2048]{1,0:T(8,128)(2,1)S(1)}, u32[]{:S(2)}, u32[]{:S(2)}) collective-permute-start(bf16[48,2048]{1,0:T(8,128)(2,1)S(1)} %reshape.17), channel_id=1, source_target_pairs={{0,4},{2,6},{4,0},{6,2},{1,5},{3,7},{5,1},{7,3},{8,12},{10,14},{12... | collective-permute-start | bytes 589832 | tf_op jit(solution)/shard_map/ppermute | solution.py:141
  40.9 1.2 %copy-start = (bf16[2048,256]{1,0:T(8,128)(2,1)S(1)}, bf16[2048,256]{1,0:T(8,128)(2,1)}, u32[]{:S(2)}) copy-start(bf16[2048,256]{1,0:T(8,128)(2,1)} %dir_ref) | copy-start | bytes 3145732
  51.8 3.1 %collective-permute-start.4 = (f32[32,512]{1,0:T(8,128)S(1)}, f32[32,512]{1,0:T(8,128)S(1)}, u32[]{:S(2)}, u32[]{:S(2)}) collective-permute-start(f32[32,512]{1,0:T(8,128)S(1)} %get-tuple-element.14), channel_id=1, source_target_pairs={{0,1},{1,0},{2,3},{3,2},{4,5},{5,4},{6,7},{7,6},{8,9},{9,8},{10,11... | collective-permute-start | bytes 196616 | tf_op jit(solution)/shard_map/ppermute | solution.py:141
  76.6 9.1 %collective-permute-start.5 = (f16[48,2048]{1,0:T(8,128)(2,1)S(1)}, f16[48,2048]{1,0:T(8,128)(2,1)S(1)}, u32[]{:S(2)}, u32[]{:S(2)}) collective-permute-start(f16[48,2048]{1,0:T(8,128)(2,1)S(1)} %get-tuple-element.15), channel_id=1, source_target_pairs={{0,4},{2,6},{4,0},{6,2},{1,5},{3,7},{5,1},{7,3},{8,12},{10,14},{12... | collective-permute-start | bytes 589832 | tf_op jit(solution)/shard_map/ppermute | solution.py:141
  78.8 10.7 %collective-permute-start.7 = (f16[48,2048]{1,0:T(8,128)(2,1)S(1)}, f16[48,2048]{1,0:T(8,128)(2,1)S(1)}, u32[]{:S(2)}, u32[]{:S(2)}) collective-permute-start(f16[48,2048]{1,0:T(8,128)(2,1)S(1)} %get-tuple-element.16), channel_id=1, source_target_pairs={{0,2},{2,4},{4,6},{6,0},{1,3},{3,5},{5,7},{7,1},{8,10},{10,12},{12... | collective-permute-start | bytes 589832 | tf_op jit(solution)/shard_map/ppermute | solution.py:141
  83.3 8.8 %collective-permute-start.6 = (f16[48,2048]{1,0:T(8,128)(2,1)S(1)}, f16[48,2048]{1,0:T(8,128)(2,1)S(1)}, u32[]{:S(2)}, u32[]{:S(2)}) collective-permute-start(f16[48,2048]{1,0:T(8,128)(2,1)S(1)} %get-tuple-element.17), channel_id=1, source_target_pairs={{0,6},{2,0},{4,2},{6,4},{1,7},{3,1},{5,3},{7,5},{8,14},{10,8},{12,... | collective-permute-start | bytes 589832 | tf_op jit(solution)/shard_map/ppermute | solution.py:141

commit v4 on v3

--- a/solution.py
+++ b/solution.py
@@ -8,13 +8,14 @@
 from jax.experimental.pallas import tpu as pltpu
 from jax.sharding import Mesh, PartitionSpec as P
 
+
 KNOTS = 17
 STEP = 3.0 / (KNOTS - 1)
 KNOT = [k * STEP for k in range(KNOTS)]
 TARGET = [math.exp(-0.5 * t * t) for t in KNOT]
 WEIGHT = [(0.5 if k in (0, KNOTS - 1) else 1.0) * STEP * TARGET[k] for k in range(KNOTS)]
 TURN = (6.28125, 0.0019340515136719, 1.2556659146e-06)
-TILE = 32
+TILE = 16
 F32 = jnp.float32
 BF16 = jnp.bfloat16
 LINK = jnp.float16
@@ -45,7 +46,8 @@
         unit_ref[pl.ds(i * rows, rows), :] = (w * inv).astype(BF16)
 
 
-def sums_kernel(rows_ref, unit_ref, more_ref, c_ref, s_ref, out_ref, proj_ref, acc_ref):
+def sums_kernel(first, rows_ref, unit_ref, more_ref, *refs):
+    c_ref, s_ref, out_ref, proj_ref, acc_ref = refs if first else refs[1:]
     rows, width = proj_ref.shape
     half = width // 2
     proj_ref[:, pl.ds(0, half)] = jnp.dot(rows_ref[...], unit_ref[...], preferred_element_type=F32)
@@ -71,7 +73,8 @@
             acc_ref[k] += fold(cc)
             acc_ref[KNOTS - 1 + k] += fold(sc)
 
-    out_ref[...] = jnp.sum(acc_ref[...], axis=1)
+    sums = jnp.sum(acc_ref[...], axis=1)
+    out_ref[...] = sums if first else sums + refs[0][...]
     for k in range(1, KNOTS):
         out_ref[pl.ds(k - 1, 1), :] -= rows * TARGET[k]
 
@@ -145,41 +148,49 @@
     ring, along_x, batch = lax.axis_size("z"), lax.axis_size("x"), lax.axis_size("y")
     depth, width = directions.shape
     block = embeddings.shape[0] * ring
-    rows = block * along_x
-    total_rows = float(2 * rows * batch)
+    total_rows = float(2 * block * along_x * batch)
     sds = jax.ShapeDtypeStruct
 
     held = to_all(embeddings, "z", ring).reshape(block, depth)
-    far = [turn(held, "x", by) for by in (2, 1, along_x - 1)]
-    directions, anchor = lax.optimization_barrier((directions, held))
-    units = [
-        call(unit_kernel, sds((depth, width), BF16), (), 4 * depth * width, 4 * depth * width, 1)(d)
-        for d in (directions, turn(directions, "c", 1))
-    ]
-    mine = jnp.concatenate([anchor] + far, axis=0)
-
-    c1, s1, sums = call(
-        sums_kernel,
-        (sds((rows, 2 * width), F32), sds((rows, 2 * width), F32), sds((2 * KNOTS - 2, 2 * width), F32)),
-        (pltpu.VMEM((rows, 2 * width), F32), pltpu.VMEM((2 * KNOTS - 2, 8, 2 * width), F32)),
-        4 * rows * depth * width,
-        8 * rows * depth,
-        3,
-    )(mine, *units)
+    order = (2, 1, along_x - 1)
+    rows = {0: held}
+    for by in order:
+        rows[by] = turn(held, "x", by)
+    sent, rows[0] = lax.optimization_barrier((directions, held))
+    theirs = turn(sent, "c", 1)
+    units = []
+    for columns in (directions, theirs):
+        units.append(call(unit_kernel, sds((depth, width), BF16), (), 4 * depth * width, 4 * depth * width, 1)(columns))
+
+    waves, sums = {}, ()
+    for by in (0,) + order:
+        c1, s1, total = call(
+            functools.partial(sums_kernel, not sums),
+            (sds((block, 2 * width), F32), sds((block, 2 * width), F32), sds((2 * KNOTS - 2, 2 * width), F32)),
+            (pltpu.VMEM((block, 2 * width), F32), pltpu.VMEM((2 * KNOTS - 2, 8, 2 * width), F32)),
+            4 * block * depth * width,
+            8 * block * depth,
+            3 + len(sums),
+        )(rows[by], *units, *sums)
+        waves[by], sums = (c1, s1), (total,)
+    (sums,) = sums
     swapped = turn(sums, "c", 1)
     sums = sums + jnp.concatenate([swapped[:, width:], swapped[:, :width]], axis=1)
     sums = to_all(sums.astype(LINK), "y", batch).astype(F32)
 
-    parts = call(
-        functools.partial(grad_kernel, total_rows),
-        sds((rows, depth), F32),
-        (pltpu.VMEM((rows, 2 * width), BF16), pltpu.VMEM((2 * KNOTS, 8, 2 * width), F32)),
-        4 * rows * depth * width,
-        4 * rows * depth,
-        5,
-    )(c1, s1, sums, *units).reshape(along_x, block, depth)
-    back = [turn(parts[j].astype(LINK), "x", by) for j, by in ((1, 2), (2, along_x - 1), (3, 1))]
-    part = parts[0] + sum(p.astype(F32) for p in back)
+    parts = {}
+    for by in (2, along_x - 1, 1, 0):
+        parts[by] = call(
+            functools.partial(grad_kernel, total_rows),
+            sds((block, depth), F32),
+            (pltpu.VMEM((block, 2 * width), BF16), pltpu.VMEM((2 * KNOTS, 8, 2 * width), F32)),
+            4 * block * depth * width,
+            4 * block * depth,
+            5,
+        )(*waves[by], sums, *units)
+        if by:
+            parts[by] = turn(parts[by].astype(LINK), "x", along_x - by)
+    part = sum(parts[by].astype(F32) for by in (0,) + order)
     part = part.astype(LINK).reshape(ring, -1, depth)
     part = lax.all_to_all(part, "z", 0, 0, tiled=True)
     return jnp.sum(part.astype(F32), axis=0)
@@ -189,4 +200,5 @@
     fine = Mesh(mesh.devices.reshape(8, 12, 4, 2), ("y", "z", "x", "c"))
     along = ("z", "x", "c")
     rows = P(("y",) + along, None)
+
     return jax.shard_map(local, mesh=fine, in_specs=(rows, P(None, along)), out_specs=rows, check_vma=False)

time: 109 us -> 107 us (0.982)
  waiting for transfers between devices: 14.3 us -> 7.17 us
  Pallas kernels: 5.24 us -> 9.17 us
    ppermute x8, waiting for transfers between devices: 14.3 us -> 7.17 us  [turn(): return lax.ppermute(x, axis, [(i, (i + by) % n) for i in range(n)])]
    pallas_call x2 -> x8, Pallas kernels: 4.72 us -> 8.66 us  [the longest x4 4.55 us: local(): call(functools.partial(grad_kernel, total_rows), sds((block, depth), F32)...]
  transfers between devices with their start and end apart: 8 -> 8, of which waited for: 6 -> 4; matrix products, arithmetic and copies ran while one was open for 0% -> 0% of each run, Pallas kernels for 0% -> 4%
where the time goes in v4:
time: 107 us; the launch traced here: 106 us
  blocking collectives  64.4 us (60%)
  starting transfers between devices  22.3 us (21%)
  Pallas kernels  9.17 us (9%)
  waiting for transfers between devices  7.17 us (7%)
  local copies, waits for them, and re-layouts  2.16 us (2%)
    all_to_all x2, blocking collectives, to_all(): lax.all_to_all(jnp.broadcast_to(x[None], (peers,) + x.shape), axes, 0, 0,...  48 us
    ppermute x8, starting transfers between devices, turn(): return lax.ppermute(x, axis, [(i, (i + by) % n) for i in range(n)])  22.3 us
    all_to_all x1, blocking collectives, local(): part = lax.all_to_all(part, 'z', 0, 0, tiled=True)  16.4 us
    ppermute x8, waiting for transfers between devices, turn(): return lax.ppermute(x, axis, [(i, (i + by) % n) for i in range(n)])  7.17 us
    pallas_call x4, Pallas kernels, local(): call(functools.partial(grad_kernel, total_rows), sds((block, depth), F32)...  4.55 us
    pallas_call x4, Pallas kernels, local(): call(functools.partial(sums_kernel, not sums), (sds((block, 2 * width), F...  4.11 us
  transfers between devices with their start and end apart: 8, of which 4 were waited for; matrix products, arithmetic and copies ran while one was open for 0% of the time, Pallas kernels for 4%

profile of v4, /device:TPU:6, one launch (start us, length us, event | category | flops | bytes accessed | tf_op | source)
XLA Modules:
  0.0 106.4 jit_solution(2533895141277834763)
XLA Ops:
  0.0 0.8 broadcast_in_dim.4
  0.8 28.9 %all_to_all.15 = bf16[12,4,2048]{2,1,0:T(4,128)(2,1)S(1)} all-to-all(bf16[12,4,2048]{2,1,0:T(4,128)(2,1)S(1)} %broadcast_in_dim.4), channel_id=1, replica_groups=mesh['y'=8,'z'=12,'x'=4,'c'=2] {'z'}, dimensions={0} | all-to-all | bytes 393216 | tf_op jit(solution)/shard_map/all_to_all | solution.py:139
  29.8 1.9 %collective-permute-start = (bf16[2048,256]{1,0:T(8,128)(2,1)}, bf16[2048,256]{1,0:T(8,128)(2,1)S(1)}, u32[]{:S(2)}, u32[]{:S(2)}) collective-permute-start(bf16[2048,256]{1,0:T(8,128)(2,1)} %dir_ref.1), channel_id=1, source_target_pairs={{0,1},{1,0},{2,3},{3,2},{4,5},{5,4},{6,7},{7,6},{8,9},{9,8},{10,11... | collective-permute-start | bytes 3145736 | tf_op jit(solution)/shard_map/ppermute | solution.py:144
  31.7 3.3 %collective-permute-start.3 = (bf16[48,2048]{1,0:T(8,128)(2,1)S(1)}, bf16[48,2048]{1,0:T(8,128)(2,1)S(1)}, u32[]{:S(2)}, u32[]{:S(2)}) collective-permute-start(bf16[48,2048]{1,0:T(8,128)(2,1)S(1)} %reshape.8.rows_ref), channel_id=1, source_target_pairs={{0,4},{2,6},{4,0},{6,2},{1,5},{3,7},{5,1},{7,3},{8,12},{10,14},{12... | collective-permute-start | bytes 589832 | tf_op jit(solution)/shard_map/ppermute | solution.py:144
  35.0 4.0 %collective-permute-start.2 = (bf16[48,2048]{1,0:T(8,128)(2,1)S(1)}, bf16[48,2048]{1,0:T(8,128)(2,1)S(1)}, u32[]{:S(2)}, u32[]{:S(2)}) collective-permute-start(bf16[48,2048]{1,0:T(8,128)(2,1)S(1)} %reshape.8.rows_ref), channel_id=1, source_target_pairs={{0,2},{2,4},{4,6},{6,0},{1,3},{3,5},{5,7},{7,1},{8,10},{10,12},{12... | collective-permute-start | bytes 589832 | tf_op jit(solution)/shard_map/ppermute | solution.py:144
  39.0 1.9 %collective-permute-start.1 = (bf16[48,2048]{1,0:T(8,128)(2,1)S(1)}, bf16[48,2048]{1,0:T(8,128)(2,1)S(1)}, u32[]{:S(2)}, u32[]{:S(2)}) collective-permute-start(bf16[48,2048]{1,0:T(8,128)(2,1)S(1)} %reshape.8.rows_ref), channel_id=1, source_target_pairs={{0,6},{2,0},{4,2},{6,4},{1,7},{3,1},{5,3},{7,5},{8,14},{10,8},{12,... | collective-permute-start | bytes 589832 | tf_op jit(solution)/shard_map/ppermute | solution.py:144
  40.9 0.0 copy-start
  41.0 1.2 %copy-done = bf16[2048,256]{1,0:T(8,128)(2,1)S(1)} copy-done((bf16[2048,256]{1,0:T(8,128)(2,1)S(1)}, bf16[2048,256]{1,0:T(8,128)(2,1)}, u32[]{:S(2)}) %copy-start) | copy-done | bytes 1048600
  42.2 0.3 shard_map.28.unit_ref
  42.4 0.0 collective-permute-done.dir_ref
  42.5 0.3 shard_map.29.more_ref
  42.7 1.0 shard_map.30
  43.7 0.0 collective-permute-done.3.rows_ref
  43.8 1.0 shard_map.31
  44.8 0.0 collective-permute-done.2.rows_ref
  44.8 1.0 shard_map.32
  45.8 3.0 %collective-permute-done.1.rows_ref = bf16[48,2048]{1,0:T(8,128)(2,1)S(1)} collective-permute-done((bf16[48,2048]{1,0:T(8,128)(2,1)S(1)}, bf16[48,2048]{1,0:T(8,128)(2,1)S(1)}, u32[]{:S(2)}, u32[]{:S(2)}) %collective-permute-start.1) | collective-permute-done | bytes 196640 | tf_op jit(solution)/shard_map/ppermute | solution.py:144
  48.9 1.0 shard_map.33
  49.9 1.9 %collective-permute-start.4 = (f32[32,512]{1,0:T(8,128)S(1)}, f32[32,512]{1,0:T(8,128)S(1)}, u32[]{:S(2)}, u32[]{:S(2)}) collective-permute-start(f32[32,512]{1,0:T(8,128)S(1)} %get-tuple-element.26), channel_id=1, source_target_pairs={{0,1},{1,0},{2,3},{3,2},{4,5},{5,4},{6,7},{7,6},{8,9},{9,8},{10,11... | collective-permute-start | bytes 196616 | tf_op jit(solution)/shard_map/ppermute | solution.py:144
  51.8 1.2 %collective-permute-done.4 = f32[32,512]{1,0:T(8,128)S(1)} collective-permute-done((f32[32,512]{1,0:T(8,128)S(1)}, f32[32,512]{1,0:T(8,128)S(1)}, u32[]{:S(2)}, u32[]{:S(2)}) %collective-permute-start.4) | collective-permute-done | bytes 65568 | tf_op jit(solution)/shard_map/ppermute | solution.py:144
  53.1 19.1 %all_to_all.16 = f16[8,32,512]{2,1,0:T(8,128)(2,1)S(1)} all-to-all(f16[8,32,512]{2,1,0:T(8,128)(2,1)S(1)} %broadcast_in_dim.5), channel_id=1, replica_groups=mesh['y'=8,'z'=12,'x'=4,'c'=2] {'y'}, dimensions={0} | all-to-all | bytes 524288 | tf_op jit(solution)/shard_map/all_to_all | solution.py:139
  72.2 0.1 convert_element_type.31.sums_ref
  72.3 1.1 %shard_map.37 = f32[48,2048]{1,0:T(8,128)S(1)} custom-call(f32[48,512]{1,0:T(8,128)S(1)} %get-tuple-element.31.c_ref, f32[48,512]{1,0:T(8,128)S(1)} %get-tuple-element.32.s_ref, f32[8,32,512]{2,1,0:T(8,128)S(1)} %convert_element_type.31.sums_ref, bf16[2048,256]{1,0:T(8,128)(2,1)S(1)} %shard_map.28.unit_ref, bf16[2048,256]{1,0:T(8,128)(2,1)S(1)} %shard_map.29.more_ref), custom_call_target="tpu_custom_call" | custom-call | flops 100663296 | bytes 393216 | tf_op jit(solution)/shard_map/pallas_call | solution.py:183
  73.4 1.1 %shard_map.36 = f32[48,2048]{1,0:T(8,128)S(1)} custom-call(f32[48,512]{1,0:T(8,128)S(1)} %get-tuple-element.29.c_ref, f32[48,512]{1,0:T(8,128)S(1)} %get-tuple-element.30.s_ref, f32[8,32,512]{2,1,0:T(8,128)S(1)} %convert_element_type.31.sums_ref, bf16[2048,256]{1,0:T(8,128)(2,1)S(1)} %shard_map.28.unit_ref, bf16[2048,256]{1,0:T(8,128)(2,1)S(1)} %shard_map.29.more_ref), custom_call_target="tpu_custom_call" | custom-call | flops 100663296 | bytes 393216 | tf_op jit(solution)/shard_map/pallas_call | solution.py:183
  74.6 1.1 %shard_map.35 = f32[48,2048]{1,0:T(8,128)S(1)} custom-call(f32[48,512]{1,0:T(8,128)S(1)} %get-tuple-element.27.c_ref, f32[48,512]{1,0:T(8,128)S(1)} %get-tuple-element.28.s_ref, f32[8,32,512]{2,1,0:T(8,128)S(1)} %convert_element_type.31.sums_ref, bf16[2048,256]{1,0:T(8,128)(2,1)S(1)} %shard_map.28.unit_ref, bf16[2048,256]{1,0:T(8,128)(2,1)S(1)} %shard_map.29.more_ref), custom_call_target="tpu_custom_call" | custom-call | flops 100663296 | bytes 393216 | tf_op jit(solution)/shard_map/pallas_call | solution.py:183
  75.8 2.2 %collective-permute-start.5 = (f16[48,2048]{1,0:T(8,128)(2,1)S(1)}, f16[48,2048]{1,0:T(8,128)(2,1)S(1)}, u32[]{:S(2)}, u32[]{:S(2)}) collective-permute-start(f16[48,2048]{1,0:T(8,128)(2,1)S(1)} %convert_element_type.32), channel_id=1, source_target_pairs={{0,4},{2,6},{4,0},{6,2},{1,5},{3,7},{5,1},{7,3},{8,12},{10,14},{12... | collective-permute-start | bytes 589832 | tf_op jit(solution)/shard_map/ppermute | solution.py:144
  78.0 2.7 %collective-permute-start.6 = (f16[48,2048]{1,0:T(8,128)(2,1)S(1)}, f16[48,2048]{1,0:T(8,128)(2,1)S(1)}, u32[]{:S(2)}, u32[]{:S(2)}) collective-permute-start(f16[48,2048]{1,0:T(8,128)(2,1)S(1)} %convert_element_type.34), channel_id=1, source_target_pairs={{0,6},{2,0},{4,2},{6,4},{1,7},{3,1},{5,3},{7,5},{8,14},{10,8},{12,... | collective-permute-start | bytes 589832 | tf_op jit(solution)/shard_map/ppermute | solution.py:144
  80.7 4.3 %collective-permute-start.7 = (f16[48,2048]{1,0:T(8,128)(2,1)S(1)}, f16[48,2048]{1,0:T(8,128)(2,1)S(1)}, u32[]{:S(2)}, u32[]{:S(2)}) collective-permute-start(f16[48,2048]{1,0:T(8,128)(2,1)S(1)} %convert_element_type.36), channel_id=1, source_target_pairs={{0,2},{2,4},{4,6},{6,0},{1,3},{3,5},{5,7},{7,1},{8,10},{10,12},{12... | collective-permute-start | bytes 589832 | tf_op jit(solution)/shard_map/ppermute | solution.py:144
  85.0 1.1 %shard_map.34 = f32[48,2048]{1,0:T(8,128)S(1)} custom-call(f32[48,512]{1,0:T(8,128)S(1)} %get-tuple-element.21.c_ref, f32[48,512]{1,0:T(8,128)S(1)} %get-tuple-element.22.s_ref, f32[8,32,512]{2,1,0:T(8,128)S(1)} %convert_element_type.31.sums_ref, bf16[2048,256]{1,0:T(8,128)(2,1)S(1)} %shard_map.28.unit_ref, bf16[2048,256]{1,0:T(8,128)(2,1)S(1)} %shard_map.29.more_ref), custom_call_target="tpu_custom_call" | custom-call | flops 100663296 | bytes 393216 | tf_op jit(solution)/shard_map/pallas_call | solution.py:183
  86.2 0.8 collective-permute-done.5
  87.0 2.1 %collective-permute-done.6 = f16[48,2048]{1,0:T(8,128)(2,1)S(1)} collective-permute-done((f16[48,2048]{1,0:T(8,128)(2,1)S(1)}, f16[48,2048]{1,0:T(8,128)(2,1)S(1)}, u32[]{:S(2)}, u32[]{:S(2)}) %collective-permute-start.6) | collective-permute-done | bytes 196640 | tf_op jit(solution)/shard_map/ppermute | solution.py:144
  89.1 0.0 collective-permute-done.7
  89.1 0.1 add_convert_fusion
  89.2 0.1 reshape.9
  89.3 16.4 %all_to_all.17 = f16[12,4,2048]{2,1,0:T(4,128)(2,1)S(1)} all-to-all(f16[12,4,2048]{2,1,0:T(4,128)(2,1)S(1)} %reshape.9), channel_id=1, replica_groups=mesh['y'=8,'z'=12,'x'=4,'c'=2] {'z'}, dimensions={0} | all-to-all | bytes 393216 | tf_op jit(solution)/shard_map/all_to_all | solution.py:195
  105.7 0.7 convert_reduce_fusion
  (7 shorter events, 0.2 us)
Async XLA Ops:
  29.8 12.7 %collective-permute-start = (bf16[2048,256]{1,0:T(8,128)(2,1)}, bf16[2048,256]{1,0:T(8,128)(2,1)S(1)}, u32[]{:S(2)}, u32[]{:S(2)}) collective-permute-start(bf16[2048,256]{1,0:T(8,128)(2,1)} %dir_ref.1), channel_id=1, source_target_pairs={{0,1},{1,0},{2,3},{3,2},{4,5},{5,4},{6,7},{7,6},{8,9},{9,8},{10,11... | collective-permute-start | bytes 3145736 | tf_op jit(solution)/shard_map/ppermute | solution.py:144
  31.7 12.1 %collective-permute-start.3 = (bf16[48,2048]{1,0:T(8,128)(2,1)S(1)}, bf16[48,2048]{1,0:T(8,128)(2,1)S(1)}, u32[]{:S(2)}, u32[]{:S(2)}) collective-permute-start(bf16[48,2048]{1,0:T(8,128)(2,1)S(1)} %reshape.8.rows_ref), channel_id=1, source_target_pairs={{0,4},{2,6},{4,0},{6,2},{1,5},{3,7},{5,1},{7,3},{8,12},{10,14},{12... | collective-permute-start | bytes 589832 | tf_op jit(solution)/shard_map/ppermute | solution.py:144
  35.0 9.8 %collective-permute-start.2 = (bf16[48,2048]{1,0:T(8,128)(2,1)S(1)}, bf16[48,2048]{1,0:T(8,128)(2,1)S(1)}, u32[]{:S(2)}, u32[]{:S(2)}) collective-permute-start(bf16[48,2048]{1,0:T(8,128)(2,1)S(1)} %reshape.8.rows_ref), channel_id=1, source_target_pairs={{0,2},{2,4},{4,6},{6,0},{1,3},{3,5},{5,7},{7,1},{8,10},{10,12},{12... | collective-permute-start | bytes 589832 | tf_op jit(solution)/shard_map/ppermute | solution.py:144
  39.0 9.8 %collective-permute-start.1 = (bf16[48,2048]{1,0:T(8,128)(2,1)S(1)}, bf16[48,2048]{1,0:T(8,128)(2,1)S(1)}, u32[]{:S(2)}, u32[]{:S(2)}) collective-permute-start(bf16[48,2048]{1,0:T(8,128)(2,1)S(1)} %reshape.8.rows_ref), channel_id=1, source_target_pairs={{0,6},{2,0},{4,2},{6,4},{1,7},{3,1},{5,3},{7,5},{8,14},{10,8},{12,... | collective-permute-start | bytes 589832 | tf_op jit(solution)/shard_map/ppermute | solution.py:144
  40.9 1.2 %copy-start = (bf16[2048,256]{1,0:T(8,128)(2,1)S(1)}, bf16[2048,256]{1,0:T(8,128)(2,1)}, u32[]{:S(2)}) copy-start(bf16[2048,256]{1,0:T(8,128)(2,1)} %dir_ref.1) | copy-start | bytes 3145732
  49.9 3.1 %collective-permute-start.4 = (f32[32,512]{1,0:T(8,128)S(1)}, f32[32,512]{1,0:T(8,128)S(1)}, u32[]{:S(2)}, u32[]{:S(2)}) collective-permute-start(f32[32,512]{1,0:T(8,128)S(1)} %get-tuple-element.26), channel_id=1, source_target_pairs={{0,1},{1,0},{2,3},{3,2},{4,5},{5,4},{6,7},{7,6},{8,9},{9,8},{10,11... | collective-permute-start | bytes 196616 | tf_op jit(solution)/shard_map/ppermute | solution.py:144
  75.8 11.2 %collective-permute-start.5 = (f16[48,2048]{1,0:T(8,128)(2,1)S(1)}, f16[48,2048]{1,0:T(8,128)(2,1)S(1)}, u32[]{:S(2)}, u32[]{:S(2)}) collective-permute-start(f16[48,2048]{1,0:T(8,128)(2,1)S(1)} %convert_element_type.32), channel_id=1, source_target_pairs={{0,4},{2,6},{4,0},{6,2},{1,5},{3,7},{5,1},{7,3},{8,12},{10,14},{12... | collective-permute-start | bytes 589832 | tf_op jit(solution)/shard_map/ppermute | solution.py:144
  78.0 11.1 %collective-permute-start.6 = (f16[48,2048]{1,0:T(8,128)(2,1)S(1)}, f16[48,2048]{1,0:T(8,128)(2,1)S(1)}, u32[]{:S(2)}, u32[]{:S(2)}) collective-permute-start(f16[48,2048]{1,0:T(8,128)(2,1)S(1)} %convert_element_type.34), channel_id=1, source_target_pairs={{0,6},{2,0},{4,2},{6,4},{1,7},{3,1},{5,3},{7,5},{8,14},{10,8},{12,... | collective-permute-start | bytes 589832 | tf_op jit(solution)/shard_map/ppermute | solution.py:144
  80.7 8.4 %collective-permute-start.7 = (f16[48,2048]{1,0:T(8,128)(2,1)S(1)}, f16[48,2048]{1,0:T(8,128)(2,1)S(1)}, u32[]{:S(2)}, u32[]{:S(2)}) collective-permute-start(f16[48,2048]{1,0:T(8,128)(2,1)S(1)} %convert_element_type.36), channel_id=1, source_target_pairs={{0,2},{2,4},{4,6},{6,0},{1,3},{3,5},{5,7},{7,1},{8,10},{10,12},{12... | collective-permute-start | bytes 589832 | tf_op jit(solution)/shard_map/ppermute | solution.py:144
